TPU v7x, 512 devices: a whole 4x4x16 slice. The times are simulated.
512 devices in a mesh: grp: 16 (over x, y), frm: 32 (over z, core).
Axes of the slice: x: 4, y: 4, z: 16, core: 2. Of those that a mesh axis runs over, the one named last changes fastest.
Arguments:
- query_in: bfloat16 [32, 2048, 2048], P(None, ('grp', 'frm')), may hold values from -32 to 32
- key_in: bfloat16 [32, 2048, 2048], P(None, ('grp', 'frm')), may hold values from -32 to 32
- value_in: bfloat16 [32, 2048, 2048], P(None, ('grp', 'frm')), may hold values from -6 to 6
- cotangent: bfloat16 [32, 2048, 2048], P('frm', 'grp'), may hold values from -6 to 6
- w_in: bfloat16 [16, 2048, 4096], P('grp', None, 'frm'), may hold values from -0.25 to 0.25
- w_out: bfloat16 [16, 4096, 2048], P('grp', 'frm'), may hold values from -0.125 to 0.125
- gate_probs: float32 [8, 512], replicated, may hold values from 0.5 to 1
- chosen: int32 [8, 512], replicated, may hold values from 0 to 65535, as said below
Outputs:
- grad_query: bfloat16 [32, 2048, 2048], P(None, ('grp', 'frm'))
- grad_key: bfloat16 [32, 2048, 2048], P(None, ('grp', 'frm'))
- grad_value: bfloat16 [32, 2048, 2048], P(None, ('grp', 'frm'))
Inputs may be any that keep to these rules, and one draw needn't show every extreme that they name: `chosen`: row e lists 512 distinct tokens, token t = frame * 2048 + patch. Call the tokens of 4 consecutive patches starting at a multiple of 4, over all frames, a block: an expert takes at most 2 tokens of a block, and exactly 2 of some block in every row.
All inputs are finite; a program needn't handle non-finite values.
Results may differ from a plain program's by a relative error of at most 0.025.
Values may be sent and summed in bfloat16 or wider, within the bound.
A program may use at most 64 MiB of HBM per device.

v0:
```python
import jax
import jax.numpy as jnp
from jax import lax
from jax.sharding import PartitionSpec as P

HEADS = 16
MOST = 2


root_half = 0.7071067811865476
inv_root_tau = 0.3989422804014327


def gelu_slope(pre_act):
    normal_cdf = 0.5 * (1.0 + jax.scipy.special.erf(pre_act * root_half))
    density = jnp.exp(-0.5 * pre_act * pre_act) * inv_root_tau
    return normal_cdf + pre_act * density


def body(query_in, key_in, value_in, cotangent, w_in, w_out, gate_probs, chosen):
    frames, blocks, features = query_in.shape
    head_dim = features // HEADS
    scaling = head_dim ** (-0.5)
    groups = lax.axis_size("grp")
    columns = lax.axis_size("frm")
    experts = gate_probs.shape[0]
    local_rows = frames * blocks
    cot_patch = lax.all_to_all(cotangent, "frm", split_axis=1, concat_axis=0, tiled=True)
    cot_flat = cot_patch.reshape(local_rows, features)
    query_heads = query_in.reshape(frames, blocks, HEADS, head_dim)
    key_heads = key_in.reshape(frames, blocks, HEADS, head_dim)
    value_heads = value_in.reshape(frames, blocks, HEADS, head_dim)
    scores = (
        jnp.einsum("fphd,gphd->phfg", query_heads, key_heads, preferred_element_type=jnp.float32)
        * scaling
    )
    highest = jnp.max(scores, axis=-1, keepdims=True)
    raised = jnp.exp(scores - highest)
    attn_probs = raised / jnp.sum(raised, axis=-1, keepdims=True)
    weights = attn_probs.astype(jnp.bfloat16)
    attn_out = jnp.einsum(
        "phfg,gphd->fphd", weights, value_heads, preferred_element_type=jnp.float32
    )
    attn_out = attn_out.astype(jnp.bfloat16).reshape(local_rows, features)
    patches_all = blocks * groups * columns
    frame_of = chosen // patches_all
    patch_of = chosen % patches_all
    holder = patch_of // blocks
    position = frame_of * blocks + patch_of % blocks
    myself = lax.axis_index("grp") * columns + lax.axis_index("frm")
    owned_here = (holder == myself).astype(jnp.int32)
    ranking = jnp.cumsum(owned_here, axis=1) - 1
    slot_ids = jnp.arange(MOST, dtype=jnp.int32)
    selected = owned_here[:, None, :] * (ranking[:, None, :] == slot_ids[None, :, None]).astype(
        jnp.int32
    )
    position_at = jnp.sum(selected * position[:, None, :], axis=2)
    filled = jnp.sum(selected, axis=2)
    weight_at = jnp.sum(selected.astype(jnp.float32) * gate_probs[:, None, :], axis=2)
    row_ids = jnp.arange(local_rows, dtype=jnp.int32)
    onehot = (
        (position_at[:, :, None] == row_ids[None, None, :]) & (filled[:, :, None] > 0)
    ).astype(jnp.bfloat16)
    picked_in = jnp.einsum(
        "eml,ld->emd", onehot, attn_out, preferred_element_type=jnp.float32
    ).astype(jnp.bfloat16)
    picked_cot = jnp.einsum(
        "eml,ld->emd",
        onehot,
        cot_patch.reshape(local_rows, features),
        preferred_element_type=jnp.float32,
    )
    scaled = (weight_at[:, :, None] * picked_cot).astype(jnp.bfloat16)
    stacked = jnp.stack([picked_in, scaled], axis=2)
    own_in = w_in[0]
    own_out = w_out[0]
    slot_depth = MOST
    outgoing = jnp.broadcast_to(stacked[:, None], (experts, 2, MOST, 2, features)).reshape(
        groups, MOST, 2, features
    )
    routed = jnp.broadcast_to(onehot[:, None, :, None, :], (experts, 2, MOST, 1, local_rows))
    pieces = 1
    slice_width = own_in.shape[1] // pieces
    arrived = lax.all_to_all(outgoing, "grp", split_axis=0, concat_axis=0, tiled=True)
    shard_rows = lax.all_gather(
        arrived.reshape(groups * slot_depth, 2, features), "frm", axis=0, tiled=True
    )
    row_count = shard_rows.shape[0]
    pre_act = jnp.dot(shard_rows[:, 0, :], own_in, preferred_element_type=jnp.float32)
    back_act = lax.dot_general(
        shard_rows[:, 1, :], own_out, (((1,), (1,)), ((), ())), preferred_element_type=jnp.float32
    )
    slope = (back_act * gelu_slope(pre_act)).astype(jnp.bfloat16)
    product = jnp.einsum(
        "rks,dks->rkd",
        slope.reshape(row_count, pieces, slice_width),
        own_in.reshape(features, pieces, slice_width),
        preferred_element_type=jnp.float32,
    )
    partial_value = product.reshape(row_count, pieces * features)
    summed = lax.psum_scatter(
        partial_value.astype(jnp.bfloat16), "frm", scatter_dimension=0, tiled=True
    )
    returned = lax.all_to_all(
        summed.reshape(groups, slot_depth, pieces, features),
        "grp",
        split_axis=0,
        concat_axis=0,
        tiled=True,
    )
    flat_back = returned.reshape(groups * slot_depth * pieces, features)
    flat_route = routed.reshape(groups * slot_depth * pieces, local_rows)
    added = jnp.einsum("nl,nd->ld", flat_route, flat_back, preferred_element_type=jnp.float32)
    grad_stream = (cot_flat.astype(jnp.float32) + added).astype(jnp.bfloat16)
    grad_heads = grad_stream.reshape(frames, blocks, HEADS, head_dim)
    grad_value = jnp.einsum(
        "phfg,fphd->gphd", weights, grad_heads, preferred_element_type=jnp.float32
    ).astype(jnp.bfloat16)
    grad_prob = jnp.einsum(
        "fphd,gphd->phfg", grad_heads, value_heads, preferred_element_type=jnp.float32
    )
    centre = jnp.sum(attn_probs * grad_prob, axis=-1, keepdims=True)
    grad_score = (attn_probs * (grad_prob - centre)).astype(jnp.bfloat16)
    grad_query = (
        jnp.einsum("phfg,gphd->fphd", grad_score, key_heads, preferred_element_type=jnp.float32)
        * scaling
    ).astype(jnp.bfloat16)
    grad_key = (
        jnp.einsum("phfg,fphd->gphd", grad_score, query_heads, preferred_element_type=jnp.float32)
        * scaling
    ).astype(jnp.bfloat16)
    return (
        grad_query.reshape(frames, blocks, features),
        grad_key.reshape(frames, blocks, features),
        grad_value.reshape(frames, blocks, features),
    )


def solution(mesh):
    return jax.shard_map(
        body,
        mesh=mesh,
        in_specs=(
            P(None, ("grp", "frm"), None),
            P(None, ("grp", "frm"), None),
            P(None, ("grp", "frm"), None),
            P("frm", "grp", None),
            P("grp", None, "frm"),
            P("grp", "frm", None),
            P(),
            P(),
        ),
        out_specs=(
            P(None, ("grp", "frm"), None),
            P(None, ("grp", "frm"), None),
            P(None, ("grp", "frm"), None),
        ),
        check_vma=False,
    )
```

profile of v0, /device:TPU:6, one launch (start us, length us, event | category | flops | bytes accessed | tf_op | source)
XLA Modules:
  0.0 304.6 jit_solution(10017114364561107741)
XLA Ops:
  7.2 0.0 copy-start
  7.2 1.9 copy.157
  9.1 0.0 copy-start.5
  9.1 0.0 copy-start.6
  9.1 0.5 broadcast.100
  9.6 3.7 %reduce.2 = bf16[128,2048]{1,0:T(8,128)(2,1)S(1)} reduce(bf16[128,1,2048]{2,1,0:T(2,128)(2,1)S(1)} %bitcast.72, bf16[]{:T(256)} %broadcast.100), dimensions={1}, to_apply=%bitcast.69.reduce_sub_computation | reduce | bytes 1048578
  13.3 1.2 reshape.124
  14.5 15.5 %all-to-all-start = ((bf16[32,2,4096]{2,1,0:T(2,128)(2,1)}), bf16[32,2,4096]{2,1,0:T(2,128)(2,1)S(1)}, u32[]{:S(2)}, u32[]{:S(2)}) async-start(bf16[32,2,4096]{2,1,0:T(2,128)(2,1)} %reshape.124), calls=%async_computation | async-start | bytes 1048576 | tf_op jit(solution)/shard_map/all_to_all | solution.py:28
  30.0 0.0 all-gather.2.cloned.1.call-start
  30.1 0.7 fusion.93
  30.8 1.1 reduce-window.6
  32.0 0.2 slice_reduce_fusion
  32.2 1.4 reshape.101
  33.6 1.4 reshape.102
  35.0 2.2 reshape.106
  37.2 0.9 fusion.83
  38.1 0.0 copy-start.1
  38.1 1.0 copy-done.1
  39.2 1.5 fusion.14
  40.7 0.2 copy.92
  40.9 0.2 reshape.116
  41.2 0.0 copy-done.5
  41.2 0.1 add_bitcast_fusion
  41.3 0.0 copy-done.6
  41.3 0.1 fusion.51
  41.4 0.2 select_reduce_fusion
  41.6 0.2 fusion.5
  41.8 22.0 %all-to-all-done = bf16[32,2,4096]{2,1,0:T(2,128)(2,1)S(1)} async-done(((bf16[32,2,4096]{2,1,0:T(2,128)(2,1)}), bf16[32,2,4096]{2,1,0:T(2,128)(2,1)S(1)}, u32[]{:S(2)}, u32[]{:S(2)}) %all-to-all-start) | async-done | bytes 524320 | tf_op jit(solution)/shard_map/all_to_all | solution.py:28
  63.8 0.5 reshape.125
  64.4 0.0 copy-start.3
  64.4 0.4 fusion.6
  64.8 0.1 copy.93
  64.9 0.2 broadcast_in_dim.8
  65.1 13.8 %all_to_all.19 = bf16[16,2,2,2048]{3,1,2,0:T(2,128)(2,1)S(1)} all-to-all(bf16[16,2,2,2048]{3,1,2,0:T(2,128)(2,1)S(1)} %bitcast.73), channel_id=1, replica_groups=mesh['grp'=16,'frm'=32] {'grp'}, dimensions={0} | all-to-all | bytes 524288 | tf_op jit(solution)/shard_map/all_to_all | solution.py:84
  78.9 0.2 copy.94
  79.1 0.8 reshape.109
  79.9 0.0 all-gather.2.cloned.1.call-update
  79.9 0.2 reduce-scatter.2.cloned.1.call-start
  80.2 68.6 %all-gather.2.cloned.1.call-done = bf16[1024,2,2048]{2,0,1:T(8,128)(2,1)} async-done(((bf16[32,2,2048]{2,0,1:T(8,128)(2,1)}), bf16[1024,2,2048]{2,0,1:T(8,128)(2,1)}) %all-gather.2.cloned.1.call-update) | async-done | bytes 8388624 | tf_op jit(solution)/shard_map/all_gather | solution.py:85
  148.7 0.0 copy-done
  148.7 4.2 %fusion.1 = f32[1024,128]{1,0:T(8,128)} fusion(bf16[1024,2,2048]{2,0,1:T(8,128)(2,1)} %all-gather.2.cloned.1.call-done, bf16[1,2048,128]{2,1,0:T(8,128)(2,1)S(1)} %copy-done), kind=kOutput, calls=%fused_computation.2 | convolution fusion | flops 536870912 | bytes 5242880 | tf_op jit(solution)/shard_map/dot_general | solution.py:89
  152.9 0.0 copy-done.3
  152.9 8.6 %convolution_convert_fusion = bf16[1024,2048]{1,0:T(8,128)(2,1)} fusion(bf16[1024,2,2048]{2,0,1:T(8,128)(2,1)} %all-gather.2.cloned.1.call-done, f32[1024,128]{1,0:T(8,128)} %fusion.1, bf16[1,2048,128]{2,1,0:T(8,128)(2,1)S(1)} %copy-done, bf16[1,128,2048]{2,1,0:T(8,128)(2,1)S(1)} %copy-done.3), kind=kOutput, calls=%fused_computation.5 | convolution fusion | flops 1077149696 | bytes 9961472 | tf_op jit(solution)/shard_map/rks,dks->rkd/dot_general | solution.py:94
  161.6 0.0 reduce-scatter.2.cloned.1.call-update
  161.6 112.1 %reduce-scatter.2.cloned.1.call-done = bf16[32,2048]{1,0:T(8,128)(2,1)} async-done(((bf16[1024,2048]{1,0:T(8,128)(2,1)}), bf16[32,2048]{1,0:T(8,128)(2,1)}) %reduce-scatter.2.cloned.1.call-update) | async-done | bytes 131088 | tf_op jit(solution)/shard_map/reduce_scatter | solution.py:101
  273.7 1.7 reshape.110
  275.4 7.3 %all-to-all-start.2 = ((bf16[16,2,1,2048]{3,1,2,0:T(2,128)(2,1)}), bf16[16,2,1,2048]{3,1,2,0:T(2,128)(2,1)S(1)}, u32[]{:S(2)}, u32[]{:S(2)}) async-start(bf16[16,2,1,2048]{3,1,2,0:T(2,128)(2,1)} %bitcast.11), calls=%async_computation.3 | async-start | bytes 262144 | tf_op jit(solution)/shard_map/all_to_all | solution.py:104
  282.6 0.1 fusion.63
  282.7 5.8 %all-to-all-done.2 = bf16[16,2,1,2048]{3,1,2,0:T(2,128)(2,1)S(1)} async-done(((bf16[16,2,1,2048]{3,1,2,0:T(2,128)(2,1)}), bf16[16,2,1,2048]{3,1,2,0:T(2,128)(2,1)S(1)}, u32[]{:S(2)}, u32[]{:S(2)}) %all-to-all-start.2) | async-done | bytes 131104 | tf_op jit(solution)/shard_map/all_to_all | solution.py:104
  288.5 0.1 reshape.111
  288.6 0.0 copy-start.2
  288.6 0.5 fusion.13
  289.1 0.1 copy.118
  289.2 1.7 fusion.15
  290.9 2.1 multiply_reduce_fusion
  293.0 0.3 multiply_convert_fusion
  293.4 0.5 fusion.11
  293.9 0.5 fusion.12
  294.4 0.2 copy.112
  294.6 0.9 reshape.122
  295.5 0.2 copy.111
  295.7 0.9 reshape.121
  296.6 0.2 copy.110
  296.8 0.9 reshape.120
  (11 shorter events, 0.1 us)
Async XLA Ops:
  7.2 141.5 %copy-start = (bf16[1,2048,128]{2,1,0:T(8,128)(2,1)S(1)}, bf16[1,2048,128]{2,1,0:T(8,128)(2,1)}, u32[]{:S(2)}) copy-start(bf16[1,2048,128]{2,1,0:T(8,128)(2,1)} %param.12) | copy-start | bytes 1572868
  9.1 32.1 %copy-start.5 = (s32[8,512]{1,0:T(8,128)S(1)}, s32[8,512]{1,0:T(8,128)}, u32[]{:S(2)}) copy-start(s32[8,512]{1,0:T(8,128)} %param.15) | copy-start | bytes 49156
  9.1 32.2 %copy-start.6 = (f32[8,512]{1,0:T(8,128)S(1)}, f32[8,512]{1,0:T(8,128)}, u32[]{:S(2)}) copy-start(f32[8,512]{1,0:T(8,128)} %param.14) | copy-start | bytes 49156
  14.5 49.3 %all-to-all-start = ((bf16[32,2,4096]{2,1,0:T(2,128)(2,1)}), bf16[32,2,4096]{2,1,0:T(2,128)(2,1)S(1)}, u32[]{:S(2)}, u32[]{:S(2)}) async-start(bf16[32,2,4096]{2,1,0:T(2,128)(2,1)} %reshape.124), calls=%async_computation | async-start | bytes 1048576 | tf_op jit(solution)/shard_map/all_to_all | solution.py:28
  30.0 118.7 %all-gather.2.cloned.1.call-start = ((), (), s32[]{:S(2)}) async-start(), calls=%async_computation.4 | async-start | bytes 8650752 | tf_op jit(solution)/shard_map/all_gather | solution.py:85
  38.1 1.1 copy-start.1
  64.4 88.6 %copy-start.3 = (bf16[1,128,2048]{2,1,0:T(8,128)(2,1)S(1)}, bf16[1,128,2048]{2,1,0:T(8,128)(2,1)}, u32[]{:S(2)}) copy-start(bf16[1,128,2048]{2,1,0:T(8,128)(2,1)} %param.13) | copy-start | bytes 1572868
  79.9 193.8 %reduce-scatter.2.cloned.1.call-start = ((), (), s32[]{:S(2)}) async-start(), calls=%async_computation.5 | async-start | bytes 4325376 | tf_op jit(solution)/shard_map/reduce_scatter | solution.py:101
  161.6 129.4 %copy-start.4 = (bf16[32,4,16,128]{3,2,1,0:T(8,128)(2,1)S(1)}, bf16[32,4,16,128]{3,2,1,0:T(8,128)(2,1)}, u32[]{:S(2)}) copy-start(bf16[32,4,16,128]{3,2,1,0:T(8,128)(2,1)} %reshape.106) | copy-start | bytes 1572868
  275.4 13.1 %all-to-all-start.2 = ((bf16[16,2,1,2048]{3,1,2,0:T(2,128)(2,1)}), bf16[16,2,1,2048]{3,1,2,0:T(2,128)(2,1)S(1)}, u32[]{:S(2)}, u32[]{:S(2)}) async-start(bf16[16,2,1,2048]{3,1,2,0:T(2,128)(2,1)} %bitcast.11), calls=%async_computation.3 | async-start | bytes 262144 | tf_op jit(solution)/shard_map/all_to_all | solution.py:104
  288.6 4.5 %copy-start.2 = (f32[4,16,32,32]{2,3,1,0:T(8,128)S(1)}, f32[4,16,32,32]{2,3,1,0:T(8,128)}, u32[]{:S(2)}) copy-start(f32[4,16,32,32]{2,3,1,0:T(8,128)} %copy-done.1) | copy-start | bytes 786436
Sparse Core Ops, SparseCore 0:
  80.0 68.6 all-gather.1
  161.7 111.9 reduce-scatter.1
where the time goes:
time: 306 us; the launch traced here: 305 us
  waiting for transfers between devices  208 us (68%)
  starting transfers between devices  23 us (8%)
  matrix products  21.2 us (7%)
  local copies, waits for them, and re-layouts  17.3 us (6%)
  between operations  14.3 us (5%)
  blocking collectives  13.8 us (5%)
  other arithmetic  6.44 us (2%)
    reduce_scatter x1, waiting for transfers between devices, body(): lax.psum_scatter(partial_value.astype(jnp.bfloat16), 'frm', scatter_dimen...  112 us
    all_gather x1, waiting for transfers between devices, body(): lax.all_gather(arrived.reshape(groups * slot_depth, 2, features), 'frm',...  68.6 us
    all_to_all x1, waiting for transfers between devices, body(): lax.all_to_all(cotangent, 'frm', split_axis=1, concat_axis=0, tiled=True)  22 us
    all_to_all x1, starting transfers between devices, body(): lax.all_to_all(cotangent, 'frm', split_axis=1, concat_axis=0, tiled=True)  15.5 us
    all_to_all x1, blocking collectives, body(): lax.all_to_all(outgoing, 'grp', split_axis=0, concat_axis=0, tiled=True)  13.8 us
    unnamed x25, local copies, waits for them, and re-layouts  8.7 us
    dot_general x1, matrix products, body(): jnp.einsum('rks,dks->rkd', slope.reshape(row_count, pieces, slice_width),...  8.62 us
    all_to_all x1, starting transfers between devices, body(): lax.all_to_all(summed.reshape(groups, slot_depth, pieces, features), 'grp...  7.27 us
  transfers between devices with their start and end apart: 4, of which 4 were waited for; matrix products, arithmetic and copies ran while one was open for 4% of the time, Pallas kernels for 0%

commit v1 on v0

--- a/solution.py
+++ b/solution.py
@@ -1,20 +1,351 @@
+import functools
+
 import jax
 import jax.numpy as jnp
 from jax import lax
+from jax.experimental import pallas as pl
+from jax.experimental.pallas import tpu as pltpu
 from jax.sharding import PartitionSpec as P
 
 HEADS = 16
 MOST = 2
-
+MESH = pl.DeviceIdType.MESH
 
 root_half = 0.7071067811865476
 inv_root_tau = 0.3989422804014327
 
 
 def gelu_slope(pre_act):
-    normal_cdf = 0.5 * (1.0 + jax.scipy.special.erf(pre_act * root_half))
+    normal_cdf = 0.5 * (1.0 + lax.erf(pre_act * root_half))
     density = jnp.exp(-0.5 * pre_act * pre_act) * inv_root_tau
     return normal_cdf + pre_act * density
+
+
+NT_DIMS = (((1,), (1,)), ((), ()))
+
+
+def expert_kernel(
+    levels,
+    rows_ref, w_in_ref, w_out_ref, out_ref,
+    gathered, w1, w2, own, x_send, x_recv, slopes, parts, cross, ring_in, ring_out,
+    last_in, last_total, last_cross,
+    local_sem, weight_send, weight_recv, first_send, first_recv,
+    ring_send, ring_recv, core_send, core_recv, x_send_sem, x_recv_sem,
+    slope_send, slope_recv, part_send, part_recv, back_send, back_recv, last_send, last_recv,
+):
+    steps = levels // 2
+    share = rows_ref.shape[1]
+    block = 2 * share
+    half = rows_ref.shape[2]
+    hidden = w_in_ref.shape[1]
+    grp = lax.axis_index("grp")
+    frm = lax.axis_index("frm")
+    side = lax.rem(grp, 2)
+    core = lax.rem(frm, 2)
+    level = lax.div(frm, 2)
+    turn = 1 - 2 * core
+    ahead = (grp, lax.rem(level + turn + levels, levels) * 2 + core)
+    behind = (grp, lax.rem(level - turn + levels, levels) * 2 + core)
+    twin = (grp, frm + turn)
+    mate = (grp + 1 - 2 * side, frm)
+
+    def remote(src, dst, send, recv, device):
+        return pltpu.make_async_remote_copy(
+            src_ref=src, dst_ref=dst, send_sem=send, recv_sem=recv, device_id=device, device_id_type=MESH
+        )
+
+    barrier = pltpu.get_barrier_semaphore()
+    for other in (ahead, behind, twin, mate):
+        pl.semaphore_signal(barrier, inc=1, device_id=other, device_id_type=MESH)
+
+    mine = pl.ds(pl.multiple_of(side * half, half), half)
+    theirs = pl.ds(pl.multiple_of((1 - side) * half, half), half)
+    here = pl.ds(pl.multiple_of(core * share, share), share)
+    lane = pl.ds(pl.multiple_of(core * block, block), block)
+    other_lane = pl.ds(pl.multiple_of((1 - core) * block, block), block)
+    lane_part = pl.ds(pl.multiple_of(core * (block + share), share), share)
+    far = pl.ds(pl.multiple_of(block + core * share, share), share)
+    other_far = pl.ds(pl.multiple_of(block + (1 - core) * share, share), share)
+    last = steps - 1
+
+    local = [
+        pltpu.make_async_copy(rows_ref.at[0], gathered.at[0, last, here], local_sem.at[0]),
+        pltpu.make_async_copy(rows_ref.at[1], gathered.at[1, last, here], local_sem.at[1]),
+        pltpu.make_async_copy(w_in_ref.at[mine], w1.at[:, pl.ds(0, hidden)], local_sem.at[2]),
+        pltpu.make_async_copy(w_out_ref.at[:, mine], w2.at[pl.ds(0, hidden)], local_sem.at[3]),
+    ]
+    for copy in local:
+        copy.start()
+    ring_in[last - 1] = jnp.zeros(ring_in.shape[1:], ring_in.dtype)
+
+    pl.semaphore_wait(barrier, 4)
+
+    first = [
+        remote(rows_ref.at[a], gathered.at[a, last, here], first_send.at[a], first_recv.at[a], twin)
+        for a in range(2)
+    ]
+    for copy in first:
+        copy.start()
+    weights = [
+        remote(w_in_ref.at[theirs], w1.at[:, pl.ds(hidden, hidden)], weight_send.at[0], weight_recv.at[0], mate),
+        remote(w_out_ref.at[:, theirs], w2.at[pl.ds(hidden, hidden)], weight_send.at[1], weight_recv.at[1], mate),
+    ]
+    for copy in weights:
+        copy.start()
+
+    def ring(t, a):
+        return remote(
+            gathered.at[a, lax.max(t - 1, 0), lane], gathered.at[a, t, lane], ring_send.at[t, a], ring_recv.at[t, a], ahead
+        )
+
+    def ring_first(a):
+        return remote(
+            gathered.at[a, last, pl.ds(0, block)], gathered.at[a, 0, lane],
+            ring_send.at[0, a], ring_recv.at[0, a], ahead,
+        )
+
+    def ring_last(a):
+        return remote(
+            gathered.at[a, last - 1, lane_part], gathered.at[a, last, far],
+            ring_send.at[last, a], ring_recv.at[last, a], ahead,
+        )
+
+    def core_copy(t, a):
+        return remote(
+            gathered.at[a, t, lane], gathered.at[a, t, lane], core_send.at[t, a], core_recv.at[t, a], twin
+        )
+
+    def core_last(a):
+        return remote(
+            gathered.at[a, last, far], gathered.at[a, last, far],
+            core_send.at[last, a], core_recv.at[last, a], twin,
+        )
+
+    def x_copy(t):
+        return remote(x_send.at[t], x_recv.at[t], x_send_sem.at[t], x_recv_sem.at[t], mate)
+
+    def slope_copy(t):
+        return remote(
+            slopes.at[t, :, pl.ds(0, hidden)], slopes.at[t, :, pl.ds(hidden, hidden)],
+            slope_send.at[t], slope_recv.at[t], mate,
+        )
+
+    def part_copy(t):
+        return remote(parts.at[t, other_lane], cross.at[t], part_send.at[t], part_recv.at[t], twin)
+
+    def part_last():
+        return remote(
+            parts.at[last, other_far], cross.at[last, pl.ds(0, share)],
+            part_send.at[last], part_recv.at[last], twin,
+        )
+
+    for a in range(2):
+        local[a].wait()
+        first[a].wait_recv()
+        ring_first(a).start()
+    for copy in local[2:]:
+        copy.wait()
+
+    def multiply(t):
+        pre = jnp.dot(gathered[0, t], w1[...], preferred_element_type=jnp.float32)
+        own[t, 0] = pre[:, :hidden]
+        x_send[t, 0] = pre[:, hidden:].astype(jnp.bfloat16)
+        back = lax.dot_general(gathered[1, t], w2[...], NT_DIMS, preferred_element_type=jnp.float32)
+        own[t, 1] = back[:, :hidden]
+        x_send[t, 1] = back[:, hidden:].astype(jnp.bfloat16)
+        x_copy(t).start()
+
+    def bend(t):
+        x_copy(t).wait_recv()
+        pre = own[t, 0] + x_recv[t, 0].astype(jnp.float32)
+        back = own[t, 1] + x_recv[t, 1].astype(jnp.float32)
+        slopes[t, :, pl.ds(0, hidden)] = (back * gelu_slope(pre)).astype(jnp.bfloat16)
+        slope_copy(t).start()
+
+    def project(t):
+        slope_copy(t).wait_recv()
+        parts[t] = lax.dot_general(
+            slopes[t], w1[...], NT_DIMS, preferred_element_type=jnp.float32
+        ).astype(jnp.bfloat16)
+
+        @pl.when(t < last)
+        def _():
+            part_copy(t).start()
+
+        @pl.when(t == last)
+        def _():
+            part_last().start()
+
+    @pl.loop(0, steps + 2)
+    def _(i):
+        @pl.when(i < last)
+        def _():
+            for a in range(2):
+                ring(i, a).wait_recv()
+
+                @pl.when(i < last - 1)
+                def _():
+                    ring(i + 1, a).start()
+
+                @pl.when(i == last - 1)
+                def _():
+                    ring_last(a).start()
+
+                core_copy(i, a).start()
+
+        @pl.when(i == last)
+        def _():
+            for a in range(2):
+                ring_last(a).wait_recv()
+                core_last(a).start()
+
+        @pl.when(i >= 2)
+        def _():
+            project(i - 2)
+
+        @pl.when((i >= 1) & (i < steps + 1))
+        def _():
+            bend(i - 1)
+
+        @pl.when(i == 0)
+        def _():
+            for copy in weights:
+                copy.wait()
+
+        @pl.when(i < last)
+        def _():
+            for a in range(2):
+                core_copy(i, a).wait_recv()
+
+        @pl.when(i == last)
+        def _():
+            for a in range(2):
+                core_last(a).wait_recv()
+
+        @pl.when(i < steps)
+        def _():
+            multiply(i)
+
+    def chunk_of(q):
+        where = (1 - core) if q == 0 else core
+        return where * share
+
+    def back_copy(t, q):
+        chunk = pl.ds(pl.multiple_of(chunk_of(q), share), share)
+        return remote(ring_out.at[t, chunk], ring_in.at[t - 1, chunk], back_send.at[t, q], back_recv.at[t, q], behind)
+
+    def back_final(q):
+        chunk = pl.ds(pl.multiple_of(chunk_of(q), share), share)
+        return remote(ring_out.at[0, chunk], last_in.at[chunk], back_send.at[0, q], back_recv.at[0, q], behind)
+
+    part_last().wait_recv()
+    total = parts[last, far].astype(jnp.float32) + cross[last, pl.ds(0, share)].astype(jnp.float32)
+    ring_out[last, here] = total.astype(jnp.bfloat16)
+    back_copy(last, 1).start()
+
+    @pl.loop(0, last)
+    def _(i):
+        t = last - 1 - i
+        part_copy(t).wait_recv()
+        for q in range(2):
+            chunk = pl.ds(pl.multiple_of(chunk_of(q), share), share)
+            source = pl.ds(pl.multiple_of(core * block + chunk_of(q), share), share)
+            if q == 0:
+                @pl.when(i > 0)
+                def _():
+                    back_copy(t + 1, 0).wait_recv()
+            else:
+                back_copy(t + 1, 1).wait_recv()
+            total = parts[t, source].astype(jnp.float32) + cross[t, chunk].astype(jnp.float32)
+            ring_out[t, chunk] = (total + ring_in[t, chunk].astype(jnp.float32)).astype(jnp.bfloat16)
+
+            @pl.when(t > 0)
+            def _():
+                back_copy(t, q).start()
+
+            @pl.when(t == 0)
+            def _():
+                back_final(q).start()
+
+    there = pl.ds(pl.multiple_of((1 - core) * share, share), share)
+    final = remote(last_total, last_cross, last_send.at[0], last_recv.at[0], twin)
+    back_final(0).wait_recv()
+    last_total[...] = (
+        parts[last, there].astype(jnp.float32) + last_in[there].astype(jnp.float32)
+    ).astype(jnp.bfloat16)
+    final.start()
+    back_final(1).wait_recv()
+    total = parts[last, here].astype(jnp.float32) + last_in[here].astype(jnp.float32)
+    final.wait_recv()
+    out_ref[...] = (total + last_cross[...].astype(jnp.float32)).astype(jnp.bfloat16)
+
+    for a in range(2):
+        first[a].wait_send()
+        ring_first(a).wait_send()
+        ring_last(a).wait_send()
+        core_last(a).wait_send()
+        back_final(a).wait_send()
+    part_last().wait_send()
+    back_copy(last, 1).wait_send()
+    final.wait_send()
+
+    @pl.loop(0, steps)
+    def _(t):
+        x_copy(t).wait_send()
+        slope_copy(t).wait_send()
+
+        @pl.when(t < last)
+        def _():
+            part_copy(t).wait_send()
+            for a in range(2):
+                core_copy(t, a).wait_send()
+
+        @pl.when((t > 0) & (t < last))
+        def _():
+            for a in range(2):
+                ring(t, a).wait_send()
+                back_copy(t, a).wait_send()
+
+
+def experts(rows, w_in, w_out):
+    levels = lax.axis_size("frm") // 2
+    steps = levels // 2
+    _, share, half = rows.shape
+    block = 2 * share
+    hidden = w_in.shape[1]
+    bf16 = jnp.bfloat16
+    dma = pltpu.SemaphoreType.DMA
+    vmem = pl.BlockSpec(memory_space=pltpu.VMEM)
+    return pl.pallas_call(
+        functools.partial(expert_kernel, levels),
+        out_shape=jax.ShapeDtypeStruct((share, half), bf16),
+        in_specs=[vmem] * 3,
+        out_specs=vmem,
+        scratch_shapes=[
+            pltpu.VMEM((2, steps, 2 * block, half), bf16),
+            pltpu.VMEM((half, 2 * hidden), bf16),
+            pltpu.VMEM((2 * hidden, half), bf16),
+            pltpu.VMEM((steps, 2, 2 * block, hidden), jnp.float32),
+            pltpu.VMEM((steps, 2, 2 * block, hidden), bf16),
+            pltpu.VMEM((steps, 2, 2 * block, hidden), bf16),
+            pltpu.VMEM((steps, 2 * block, 2 * hidden), bf16),
+            pltpu.VMEM((steps, 2 * block, half), bf16),
+            pltpu.VMEM((steps, block, half), bf16),
+            pltpu.VMEM((steps, block, half), bf16),
+            pltpu.VMEM((steps, block, half), bf16),
+            pltpu.VMEM((block, half), bf16),
+            pltpu.VMEM((share, half), bf16),
+            pltpu.VMEM((share, half), bf16),
+            dma((4,)), dma((2,)), dma((2,)), dma((2,)), dma((2,)),
+            dma((steps, 2)), dma((steps, 2)), dma((steps, 2)), dma((steps, 2)),
+            dma((steps,)), dma((steps,)), dma((steps,)), dma((steps,)),
+            dma((steps,)), dma((steps,)), dma((steps, 2)), dma((steps, 2)), dma((1,)), dma((1,)),
+        ],
+        compiler_params=pltpu.CompilerParams(
+            collective_id=0, has_side_effects=True, vmem_limit_bytes=48 * 1024 * 1024
+        ),
+        name="experts",
+    )(rows, w_in, w_out)
 
 
 def body(query_in, key_in, value_in, cotangent, w_in, w_out, gate_probs, chosen):
@@ -23,7 +354,8 @@
     scaling = head_dim ** (-0.5)
     groups = lax.axis_size("grp")
     columns = lax.axis_size("frm")
-    experts = gate_probs.shape[0]
+    experts_total = gate_probs.shape[0]
+    half = features // 2
     local_rows = frames * blocks
     cot_patch = lax.all_to_all(cotangent, "frm", split_axis=1, concat_axis=0, tiled=True)
     cot_flat = cot_patch.reshape(local_rows, features)
@@ -64,52 +396,20 @@
     picked_in = jnp.einsum(
         "eml,ld->emd", onehot, attn_out, preferred_element_type=jnp.float32
     ).astype(jnp.bfloat16)
-    picked_cot = jnp.einsum(
-        "eml,ld->emd",
-        onehot,
-        cot_patch.reshape(local_rows, features),
-        preferred_element_type=jnp.float32,
-    )
+    picked_cot = jnp.einsum("eml,ld->emd", onehot, cot_flat, preferred_element_type=jnp.float32)
     scaled = (weight_at[:, :, None] * picked_cot).astype(jnp.bfloat16)
-    stacked = jnp.stack([picked_in, scaled], axis=2)
-    own_in = w_in[0]
-    own_out = w_out[0]
-    slot_depth = MOST
-    outgoing = jnp.broadcast_to(stacked[:, None], (experts, 2, MOST, 2, features)).reshape(
-        groups, MOST, 2, features
-    )
-    routed = jnp.broadcast_to(onehot[:, None, :, None, :], (experts, 2, MOST, 1, local_rows))
-    pieces = 1
-    slice_width = own_in.shape[1] // pieces
+    stacked = jnp.stack([picked_in, scaled], axis=1)
+    outgoing = stacked.reshape(experts_total, 2, MOST, 2, half).transpose(0, 3, 1, 2, 4)
+    outgoing = outgoing.reshape(groups, 2, MOST, half)
     arrived = lax.all_to_all(outgoing, "grp", split_axis=0, concat_axis=0, tiled=True)
-    shard_rows = lax.all_gather(
-        arrived.reshape(groups * slot_depth, 2, features), "frm", axis=0, tiled=True
-    )
-    row_count = shard_rows.shape[0]
-    pre_act = jnp.dot(shard_rows[:, 0, :], own_in, preferred_element_type=jnp.float32)
-    back_act = lax.dot_general(
-        shard_rows[:, 1, :], own_out, (((1,), (1,)), ((), ())), preferred_element_type=jnp.float32
-    )
-    slope = (back_act * gelu_slope(pre_act)).astype(jnp.bfloat16)
-    product = jnp.einsum(
-        "rks,dks->rkd",
-        slope.reshape(row_count, pieces, slice_width),
-        own_in.reshape(features, pieces, slice_width),
-        preferred_element_type=jnp.float32,
-    )
-    partial_value = product.reshape(row_count, pieces * features)
-    summed = lax.psum_scatter(
-        partial_value.astype(jnp.bfloat16), "frm", scatter_dimension=0, tiled=True
-    )
+    rows = arrived.transpose(1, 0, 2, 3).reshape(2, groups * MOST, half)
+    summed = experts(rows, w_in[0], w_out[0])
     returned = lax.all_to_all(
-        summed.reshape(groups, slot_depth, pieces, features),
-        "grp",
-        split_axis=0,
-        concat_axis=0,
-        tiled=True,
-    )
-    flat_back = returned.reshape(groups * slot_depth * pieces, features)
-    flat_route = routed.reshape(groups * slot_depth * pieces, local_rows)
+        summed.reshape(groups, MOST, half), "grp", split_axis=0, concat_axis=0, tiled=True
+    )
+    flat_back = returned.reshape(experts_total, 2, MOST, half).transpose(0, 2, 1, 3)
+    flat_back = flat_back.reshape(experts_total * MOST, features)
+    flat_route = onehot.reshape(experts_total * MOST, local_rows)
     added = jnp.einsum("nl,nd->ld", flat_route, flat_back, preferred_element_type=jnp.float32)
     grad_stream = (cot_flat.astype(jnp.float32) + added).astype(jnp.bfloat16)
     grad_heads = grad_stream.reshape(frames, blocks, HEADS, head_dim)

time: 306 us -> 169 us (0.55)
  waiting for transfers between devices: 208 us -> 30.4 us
  Pallas kernels: 0 us -> 76.5 us
  matrix products: 21.2 us -> 4.98 us
  between operations: 14.3 us -> 0.93 us
    reduce_scatter x1 -> x0, waiting for transfers between devices: 112 us -> none  [body(): lax.psum_scatter(partial_value.astype(jnp.bfloat16), 'frm', scatter_dimen...]
    pallas_call x0 -> x1, Pallas kernels: none -> 76.5 us  [experts(): pl.pallas_call(functools.partial(expert_kernel, levels), out_shape=jax.Sh...]
    all_gather x1 -> x0, waiting for transfers between devices: 68.6 us -> none  [body(): lax.all_gather(arrived.reshape(groups * slot_depth, 2, features), 'frm',...]
    dot_general x3 -> x1, matrix products: 13.2 us -> 0.4 us  [body(): jnp.einsum('eml,ld->emd', onehot, cot_flat, preferred_element_type=jnp.fl...]
    all_to_all x1, waiting for transfers between devices: 22 us -> 25.1 us  [body(): lax.all_to_all(cotangent, 'frm', split_axis=1, concat_axis=0, tiled=True)]
    unnamed x25 -> x36, local copies, waits for them, and re-layouts: 8.7 us -> 11.7 us
  transfers between devices with their start and end apart: 4 -> 2, of which waited for: 4 -> 2; matrix products, arithmetic and copies ran while one was open for 4% -> 3% of each run, Pallas kernels for 0% -> 0%
where the time goes in v1:
time: 169 us; the launch traced here: 168 us
  Pallas kernels  76.5 us (45%)
  waiting for transfers between devices  30.4 us (18%)
  starting transfers between devices  21.2 us (13%)
  local copies, waits for them, and re-layouts  15.3 us (9%)
  blocking collectives  13.2 us (8%)
  other arithmetic  5.65 us (3%)
  matrix products  4.98 us (3%)
    pallas_call x1, Pallas kernels, experts(): pl.pallas_call(functools.partial(expert_kernel, levels), out_shape=jax.Sh...  76.5 us
    all_to_all x1, waiting for transfers between devices, body(): lax.all_to_all(cotangent, 'frm', split_axis=1, concat_axis=0, tiled=True)  25.1 us
    all_to_all x1, starting transfers between devices, body(): lax.all_to_all(cotangent, 'frm', split_axis=1, concat_axis=0, tiled=True)  15.6 us
    all_to_all x1, blocking collectives, body(): lax.all_to_all(outgoing, 'grp', split_axis=0, concat_axis=0, tiled=True)  13.2 us
    unnamed x36, local copies, waits for them, and re-layouts  11.7 us
    all_to_all x1, starting transfers between devices, body(): lax.all_to_all(summed.reshape(groups, MOST, half), 'grp', split_axis=0, c...  5.57 us
    all_to_all x1, waiting for transfers between devices, body(): lax.all_to_all(summed.reshape(groups, MOST, half), 'grp', split_axis=0, c...  5.3 us
    unnamed x1, other arithmetic  3.7 us
  transfers between devices with their start and end apart: 2, of which 2 were waited for; matrix products, arithmetic and copies ran while one was open for 3% of the time, Pallas kernels for 0%

profile of v1, /device:TPU:6, one launch (start us, length us, event | category | flops | bytes accessed | tf_op | source)
XLA Modules:
  0.0 168.2 jit_solution(10844347642896965436)
XLA Ops:
  0.6 1.9 %copy.185 = bf16[1,128,2048]{2,0,1:T(2,128)(2,1)S(1)} copy(bf16[1,128,2048]{2,1,0:T(8,128)(2,1)} %param.11) | data formatting | bytes 1048576 | tf_op args[3]
  2.5 0.5 broadcast.93
  3.0 3.7 %reduce.2 = bf16[128,2048]{1,0:T(8,128)(2,1)S(1)} reduce(bf16[128,1,2048]{2,1,0:T(2,128)(2,1)S(1)} %bitcast.55, bf16[]{:T(256)} %broadcast.93), dimensions={1}, to_apply=%bitcast.50.reduce_sub_computation | reduce | bytes 1048578
  6.7 1.2 reshape.119
  7.9 15.6 %all-to-all-start = ((bf16[32,2,4096]{2,1,0:T(2,128)(2,1)}), bf16[32,2,4096]{2,1,0:T(2,128)(2,1)S(1)}, u32[]{:S(2)}, u32[]{:S(2)}) async-start(bf16[32,2,4096]{2,1,0:T(2,128)(2,1)} %reshape.119), calls=%async_computation | async-start | bytes 1048576 | tf_op jit(solution)/shard_map/all_to_all | solution.py:360
  23.5 0.0 copy-done.9
  23.6 1.1 reduce-window.6
  24.7 0.2 slice_reduce_fusion
  25.0 0.0 copy-done.4
  25.0 0.0 copy-start.5
  25.0 0.3 reshape.95
  25.3 0.2 copy-done.11
  25.6 0.5 copy-done.5
  26.0 0.3 reshape.96
  26.4 0.7 copy-done.6
  27.1 0.3 reshape.100
  27.4 0.0 copy-start.7
  27.4 0.9 fusion.61
  28.4 0.0 copy-start.2
  28.4 0.0 copy-done.7
  28.4 1.0 copy-done.2
  29.4 0.5 fusion.12
  29.9 0.2 copy.119
  30.1 0.2 reshape.111
  30.3 0.0 slice-start
  30.4 0.6 slice-done
  31.0 0.1 add_bitcast_fusion
  31.1 0.6 copy-done.10
  31.7 0.1 fusion.31
  31.9 0.2 select_reduce_fusion
  32.0 0.2 fusion.3
  32.3 25.1 %all-to-all-done = bf16[32,2,4096]{2,1,0:T(2,128)(2,1)S(1)} async-done(((bf16[32,2,4096]{2,1,0:T(2,128)(2,1)}), bf16[32,2,4096]{2,1,0:T(2,128)(2,1)S(1)}, u32[]{:S(2)}, u32[]{:S(2)}) %all-to-all-start) | async-done | bytes 524320 | tf_op jit(solution)/shard_map/all_to_all | solution.py:360
  57.3 0.5 reshape.120
  57.9 0.4 fusion.4
  58.3 0.0 copy-start
  58.3 0.0 copy-start.1
  58.3 0.1 copy.120
  58.5 13.2 %all_to_all.19 = bf16[16,2,2,1024]{3,2,1,0:T(2,128)(2,1)S(1)} all-to-all(bf16[16,2,2,1024]{3,2,1,0:T(2,128)(2,1)S(1)} %bitcast.58), channel_id=1, replica_groups=mesh['grp'=16,'frm'=32] {'grp'}, dimensions={0} | all-to-all | bytes 262144 | tf_op jit(solution)/shard_map/all_to_all | solution.py:404
  71.7 0.1 copy.121
  71.8 0.1 reshape.103.rows_ref
  71.8 76.5 %experts.1 = bf16[32,1024]{1,0:T(8,128)(2,1)S(1)} custom-call(bf16[2,32,1024]{2,1,0:T(8,128)(2,1)S(1)} %reshape.103.rows_ref, bf16[2048,128]{1,0:T(8,128)(2,1)S(1)} %bitcast.51, bf16[128,2048]{1,0:T(8,128)(2,1)S(1)} %bitcast.52), custom_call_target="tpu_custom_call" | custom-call | tf_op jit(solution)/shard_map/experts/pallas_call | solution.py:319
  148.4 0.7 reshape.104
  149.1 5.6 %all-to-all-start.2 = ((bf16[16,2,1024]{2,1,0:T(2,128)(2,1)}), bf16[16,2,1024]{2,1,0:T(2,128)(2,1)S(1)}, u32[]{:S(2)}, u32[]{:S(2)}) async-start(bf16[16,2,1024]{2,1,0:T(2,128)(2,1)} %reshape.104), calls=%async_computation.2 | async-start | bytes 131072 | tf_op jit(solution)/shard_map/all_to_all | solution.py:407
  154.6 0.1 copy.115
  154.7 0.1 copy.116
  154.8 0.1 eq.49
  154.9 0.1 gt.13
  155.0 5.3 %all-to-all-done.2 = bf16[16,2,1024]{2,1,0:T(2,128)(2,1)S(1)} async-done(((bf16[16,2,1024]{2,1,0:T(2,128)(2,1)}), bf16[16,2,1024]{2,1,0:T(2,128)(2,1)S(1)}, u32[]{:S(2)}, u32[]{:S(2)}) %all-to-all-start.2) | async-done | bytes 65568 | tf_op jit(solution)/shard_map/all_to_all | solution.py:407
  160.3 0.1 copy.122
  160.4 0.6 fusion.11
  160.9 0.1 copy.146
  161.1 0.5 copy-done.3
  161.6 0.5 fusion.13
  162.1 0.6 copy-done.8
  162.6 0.9 multiply_reduce_fusion
  163.5 0.3 multiply_convert_fusion
  163.8 0.5 fusion.9
  164.3 0.5 fusion.10
  164.8 0.2 copy.139
  165.0 0.9 reshape.117
  165.9 0.2 copy.138
  166.2 0.9 reshape.116
  167.1 0.2 copy.137
  167.3 0.9 reshape.115
  (17 shorter events, 0.2 us)
Async XLA Ops:
  7.9 15.6 %copy-start.9 = (s32[8,512]{1,0:T(8,128)S(1)}, s32[8,512]{1,0:T(8,128)}, u32[]{:S(2)}) copy-start(s32[8,512]{1,0:T(8,128)} %param.15) | copy-start | bytes 49156
  7.9 17.1 %copy-start.4 = (bf16[32,4,2048]{2,1,0:T(4,128)(2,1)S(1)}, bf16[32,4,2048]{2,1,0:T(4,128)(2,1)}, u32[]{:S(2)}) copy-start(bf16[32,4,2048]{2,1,0:T(4,128)(2,1)} %param.8) | copy-start | bytes 1572868
  7.9 49.4 %all-to-all-start = ((bf16[32,2,4096]{2,1,0:T(2,128)(2,1)}), bf16[32,2,4096]{2,1,0:T(2,128)(2,1)S(1)}, u32[]{:S(2)}, u32[]{:S(2)}) async-start(bf16[32,2,4096]{2,1,0:T(2,128)(2,1)} %reshape.119), calls=%async_computation | async-start | bytes 1048576 | tf_op jit(solution)/shard_map/all_to_all | solution.py:360
  25.0 0.6 copy-start.11
  25.0 1.0 copy-start.5
  26.0 1.0 copy-start.6
  27.4 1.0 copy-start.7
  28.4 1.0 copy-start.2
  30.3 0.7 slice-start
  31.0 0.7 copy-start.10
  58.3 13.5 %copy-start = (bf16[1,2048,128]{2,1,0:T(8,128)(2,1)S(1)}, bf16[1,2048,128]{2,1,0:T(8,128)(2,1)}, u32[]{:S(2)}) copy-start(bf16[1,2048,128]{2,1,0:T(8,128)(2,1)} %param.12) | copy-start | bytes 1572868
  58.3 13.5 %copy-start.1 = (bf16[1,128,2048]{2,1,0:T(8,128)(2,1)S(1)}, bf16[1,128,2048]{2,1,0:T(8,128)(2,1)}, u32[]{:S(2)}) copy-start(bf16[1,128,2048]{2,1,0:T(8,128)(2,1)} %param.13) | copy-start | bytes 1572868
  149.1 11.2 %all-to-all-start.2 = ((bf16[16,2,1024]{2,1,0:T(2,128)(2,1)}), bf16[16,2,1024]{2,1,0:T(2,128)(2,1)S(1)}, u32[]{:S(2)}, u32[]{:S(2)}) async-start(bf16[16,2,1024]{2,1,0:T(2,128)(2,1)} %reshape.104), calls=%async_computation.2 | async-start | bytes 131072 | tf_op jit(solution)/shard_map/all_to_all | solution.py:407
  160.3 1.2 copy-start.3
  161.6 1.0 copy-start.8

commit v2 on v1

v2 whole, which is shorter than its diff:
```python
import functools

import jax
import jax.numpy as jnp
from jax import lax
from jax.experimental import pallas as pl
from jax.experimental.pallas import tpu as pltpu
from jax.sharding import PartitionSpec as P

HEADS = 16
MOST = 2
MESH = pl.DeviceIdType.MESH

root_half = 0.7071067811865476
inv_root_tau = 0.3989422804014327


def gelu_slope(pre_act):
    normal_cdf = 0.5 * (1.0 + lax.erf(pre_act * root_half))
    density = jnp.exp(-0.5 * pre_act * pre_act) * inv_root_tau
    return normal_cdf + pre_act * density


NT_DIMS = (((1,), (1,)), ((), ()))
TN_DIMS = (((0,), (0,)), ((), ()))
LAG_MID = 2
LAG_OUT = 3


def bits(n):
    assert n & (n - 1) == 0
    return n.bit_length() - 1


def onehot_rows(chosen, gates, myself, blocks, patches, local_rows):
    experts_total, cap = chosen.shape
    slots = MOST * experts_total

    def twice(values):
        spread = jnp.broadcast_to(values[:, None, :], (experts_total, MOST, cap))
        return spread.reshape(slots, cap)

    token = twice(chosen)
    gate = twice(gates)
    patch = token & (patches - 1)
    frame = lax.shift_right_logical(token, bits(patches))
    holder = lax.shift_right_logical(patch, bits(blocks))
    place = frame * blocks + (patch & (blocks - 1))
    order = lax.broadcasted_iota(jnp.int32, (slots, cap), 1)
    key = (order * local_rows + place).astype(jnp.float32)
    owned = holder == myself
    beyond = float(cap * local_rows)
    low = jnp.min(jnp.where(owned, key, beyond), axis=1, keepdims=True)
    high = jnp.max(jnp.where(owned, key, -1.0), axis=1, keepdims=True)
    odd = (lax.broadcasted_iota(jnp.int32, (slots, 1), 0) & 1) == 1
    key_at = jnp.where(odd, high, low)
    present = jnp.where(odd, (high > low).astype(jnp.float32), (low < beyond).astype(jnp.float32))
    place_at = key_at - jnp.floor(key_at * (1.0 / local_rows)) * local_rows
    gate_at = jnp.sum(jnp.where(owned & (key == key_at), gate, 0.0), axis=1, keepdims=True)
    row = lax.broadcasted_iota(jnp.int32, (slots, local_rows), 1).astype(jnp.float32)
    hit = jnp.where((row == place_at) & (present > 0.5), 1.0, 0.0)
    return hit.astype(jnp.bfloat16), gate_at


def layer_kernel(
    levels, groups, patches,
    query_ref, key_ref, value_ref, cot_ref, w_in_ref, w_out_ref, gates_ref, chosen_ref,
    probs_ref, onehot_ref, stream_ref, back_ref,
    query, key, value, mixed, cot_rows, picked, returned, final_rows,
    gathered, w1, w2, own, x_send, x_recv, slopes, parts, cross, ring_in, ring_out,
    last_in, last_total, last_cross,
    local_sem, load_sem, weight_send, weight_recv, first_send, first_recv,
    ring_send, ring_recv, core_send, core_recv, x_send_sem, x_recv_sem,
    slope_send, slope_recv, part_send, part_recv, back_send, back_recv, last_send, last_recv,
    cot_send, cot_recv, pick_send, pick_recv, return_send, return_recv,
):
    steps = levels // 2
    last = steps - 1
    columns = 2 * levels
    frames, blocks, features = query_ref.shape
    local_rows = frames * blocks
    head_dim = features // HEADS
    half = features // 2
    share = MOST * groups
    block = 2 * share
    hidden = w_in_ref.shape[1]
    grp = lax.axis_index("grp")
    frm = lax.axis_index("frm")
    side = lax.rem(grp, 2)
    expert = lax.div(grp, 2)
    core = lax.rem(frm, 2)
    level = lax.div(frm, 2)
    turn = 1 - 2 * core
    ahead = (grp, lax.rem(level + turn + levels, levels) * 2 + core)
    behind = (grp, lax.rem(level - turn + levels, levels) * 2 + core)
    twin = (grp, frm + turn)
    mate = (grp + 1 - 2 * side, frm)

    def remote(src, dst, send, recv, device):
        return pltpu.make_async_remote_copy(
            src_ref=src, dst_ref=dst, send_sem=send, recv_sem=recv, device_id=device, device_id_type=MESH
        )

    def part_of(index, size):
        return pl.ds(pl.multiple_of(index * size, size), size)

    barrier = pltpu.get_barrier_semaphore()

    @pl.loop(1, columns)
    def _(d):
        pl.semaphore_signal(
            barrier, inc=1, device_id=(grp, lax.rem(frm + d, columns)), device_id_type=MESH
        )

    @pl.loop(1, groups)
    def _(d):
        pl.semaphore_signal(
            barrier, inc=1, device_id=(lax.rem(grp + d, groups), frm), device_id_type=MESH
        )

    mine = part_of(side, half)
    theirs = part_of(1 - side, half)
    here = part_of(core, share)
    lane = part_of(core, block)
    other_lane = part_of(1 - core, block)
    lane_part = pl.ds(pl.multiple_of(core * (block + share), share), share)
    far = pl.ds(pl.multiple_of(block + core * share, share), share)
    other_far = pl.ds(pl.multiple_of(block + (1 - core) * share, share), share)

    inputs = ((query_ref, query), (key_ref, key), (value_ref, value))

    @pl.loop(0, frames)
    def _(f):
        for n, (src, dst) in enumerate(inputs):
            pltpu.make_async_copy(src.at[f], dst.at[part_of(f, blocks)], load_sem.at[n]).start()

    local = [
        pltpu.make_async_copy(w_in_ref.at[mine], w1.at[:, pl.ds(0, hidden)], local_sem.at[0]),
        pltpu.make_async_copy(w_out_ref.at[:, mine], w2.at[pl.ds(0, hidden)], local_sem.at[1]),
        pltpu.make_async_copy(
            cot_ref.at[0, part_of(frm, blocks)], cot_rows.at[part_of(frm, blocks)], local_sem.at[2]
        ),
    ]
    for copy in local:
        copy.start()
    ring_in[last - 1] = jnp.zeros(ring_in.shape[1:], ring_in.dtype)
    myself = grp * columns + frm
    onehot, gate_at = onehot_rows(chosen_ref[...], gates_ref[...], myself, blocks, patches, local_rows)
    onehot_ref[...] = onehot

    pl.semaphore_wait(barrier, columns + groups - 2)

    def cot_copy(other):
        return remote(
            cot_ref.at[0, part_of(other, blocks)], cot_rows.at[part_of(frm, blocks)],
            cot_send.at[other], cot_recv.at[frm], (grp, other),
        )

    def cot_arrival(other):
        return remote(
            cot_ref.at[0, part_of(other, blocks)], cot_rows.at[part_of(other, blocks)],
            cot_send.at[other], cot_recv.at[other], (grp, other),
        )

    @pl.loop(0, levels - 1)
    def _(k):
        away = steps - lax.div(k + 1, 2)
        to = lax.rem(level + levels + (2 * lax.rem(k, 2) - 1) * away, levels)
        cot_copy(2 * to + core).start()
        cot_copy(2 * to + 1 - core).start()

    cot_copy(frm + turn).start()
    weights = [
        remote(w_in_ref.at[theirs], w1.at[:, pl.ds(hidden, hidden)], weight_send.at[0], weight_recv.at[0], mate),
        remote(w_out_ref.at[:, theirs], w2.at[pl.ds(hidden, hidden)], weight_send.at[1], weight_recv.at[1], mate),
    ]
    for copy in weights:
        copy.start()

    for n, (_, dst) in enumerate(inputs):
        pltpu.make_async_copy(dst, dst, load_sem.at[n]).wait()
    row_patch = lax.broadcasted_iota(jnp.int32, (local_rows, local_rows), 0) & (blocks - 1)
    column_patch = lax.broadcasted_iota(jnp.int32, (local_rows, local_rows), 1) & (blocks - 1)
    same = row_patch == column_patch
    scaling = head_dim ** (-0.5)
    together = 4

    @pl.loop(0, HEADS // together)
    def _(n):
        for m in range(together):
            head = n * together + m
            cols = part_of(head, head_dim)
            scores = lax.dot_general(
                query[:, cols], key[:, cols], NT_DIMS, preferred_element_type=jnp.float32
            ) * scaling
            scores = jnp.where(same, scores, -1e30)
            raised = jnp.exp(scores - jnp.max(scores, axis=1, keepdims=True))
            probs = raised / jnp.sum(raised, axis=1, keepdims=True)
            probs_ref[head] = probs
            mixed[:, cols] = jnp.dot(
                probs.astype(jnp.bfloat16), value[:, cols], preferred_element_type=jnp.float32
            ).astype(jnp.bfloat16)

    def pick_copy(a, d):
        to = lax.rem(grp + d, groups)
        return remote(
            picked.at[a, part_of(lax.div(to, 2), MOST), part_of(lax.rem(to, 2), half)],
            gathered.at[a, last, pl.ds(pl.multiple_of(core * share + grp * MOST, MOST), MOST)],
            pick_send.at[a, to], pick_recv.at[a, grp], (to, frm),
        )

    def pick_arrival(a, d):
        to = lax.rem(grp + d, groups)
        return remote(
            picked.at[a, part_of(lax.div(to, 2), MOST), part_of(lax.rem(to, 2), half)],
            gathered.at[a, last, pl.ds(pl.multiple_of(core * share + to * MOST, MOST), MOST)],
            pick_send.at[a, to], pick_recv.at[a, to], (to, frm),
        )

    def pick_own(a):
        return pltpu.make_async_copy(
            picked.at[a, part_of(expert, MOST), part_of(side, half)],
            gathered.at[a, last, pl.ds(pl.multiple_of(core * share + grp * MOST, MOST), MOST)],
            pick_send.at[a, grp],
        )

    def first(a):
        return remote(
            gathered.at[a, last, here], gathered.at[a, last, here], first_send.at[a], first_recv.at[a], twin
        )

    def send_picked(a):
        @pl.loop(1, groups)
        def _(d):
            pick_copy(a, d).start()

        pick_own(a).start()

    def take_picked(a):
        pick_own(a).wait()

        @pl.loop(1, groups)
        def _(d):
            pick_arrival(a, d).wait_recv()

        first(a).start()
        first(a).wait_recv()
        ring_first(a).start()

    picked[0] = jnp.dot(onehot, mixed[...], preferred_element_type=jnp.float32).astype(jnp.bfloat16)
    send_picked(0)

    def ring(t, a):
        return remote(
            gathered.at[a, lax.max(t - 1, 0), lane], gathered.at[a, t, lane], ring_send.at[t, a], ring_recv.at[t, a], ahead
        )

    def ring_first(a):
        return remote(
            gathered.at[a, last, pl.ds(0, block)], gathered.at[a, 0, lane],
            ring_send.at[0, a], ring_recv.at[0, a], ahead,
        )

    def ring_last(a):
        return remote(
            gathered.at[a, last - 1, lane_part], gathered.at[a, last, far],
            ring_send.at[last, a], ring_recv.at[last, a], ahead,
        )

    def core_copy(t, a):
        return remote(
            gathered.at[a, t, lane], gathered.at[a, t, lane], core_send.at[t, a], core_recv.at[t, a], twin
        )

    def core_last(a):
        return remote(
            gathered.at[a, last, far], gathered.at[a, last, far],
            core_send.at[last, a], core_recv.at[last, a], twin,
        )

    def x_copy(t):
        return remote(x_send.at[t], x_recv.at[t], x_send_sem.at[t], x_recv_sem.at[t], mate)

    def slope_copy(t):
        return remote(
            slopes.at[t, :, pl.ds(0, hidden)], slopes.at[t, :, pl.ds(hidden, hidden)],
            slope_send.at[t], slope_recv.at[t], mate,
        )

    def part_copy(t):
        return remote(parts.at[t, other_lane], cross.at[t], part_send.at[t], part_recv.at[t], twin)

    def part_last():
        return remote(
            parts.at[last, other_far], cross.at[last, pl.ds(0, share)],
            part_send.at[last], part_recv.at[last], twin,
        )

    take_picked(0)
    local[2].wait()

    @pl.loop(1, columns)
    def _(d):
        cot_arrival(lax.rem(frm + d, columns)).wait_recv()

    picked_cot = jnp.dot(onehot, cot_rows[...], preferred_element_type=jnp.float32)
    picked[1] = (gate_at * picked_cot).astype(jnp.bfloat16)
    send_picked(1)
    stream_ref[...] = cot_rows[...]
    for copy in local[:2]:
        copy.wait()
    take_picked(1)

    def multiply(t):
        pre = jnp.dot(gathered[0, t], w1[...], preferred_element_type=jnp.float32)
        own[t, 0] = pre[:, :hidden]
        x_send[t, 0] = pre[:, hidden:].astype(jnp.bfloat16)
        back = lax.dot_general(gathered[1, t], w2[...], NT_DIMS, preferred_element_type=jnp.float32)
        own[t, 1] = back[:, :hidden]
        x_send[t, 1] = back[:, hidden:].astype(jnp.bfloat16)
        x_copy(t).start()

    def bend(t):
        x_copy(t).wait_recv()
        pre = own[t, 0] + x_recv[t, 0].astype(jnp.float32)
        back = own[t, 1] + x_recv[t, 1].astype(jnp.float32)
        slopes[t, :, pl.ds(0, hidden)] = (back * gelu_slope(pre)).astype(jnp.bfloat16)
        slope_copy(t).start()

    def project(t):
        slope_copy(t).wait_recv()
        parts[t] = lax.dot_general(
            slopes[t], w1[...], NT_DIMS, preferred_element_type=jnp.float32
        ).astype(jnp.bfloat16)

        @pl.when(t < last)
        def _():
            part_copy(t).start()

        @pl.when(t == last)
        def _():
            part_last().start()

    @pl.loop(0, steps + LAG_OUT)
    def _(i):
        @pl.when(i < last)
        def _():
            for a in range(2):
                ring(i, a).wait_recv()

                @pl.when(i < last - 1)
                def _():
                    ring(i + 1, a).start()

                @pl.when(i == last - 1)
                def _():
                    ring_last(a).start()

                core_copy(i, a).start()

        @pl.when(i == last)
        def _():
            for a in range(2):
                ring_last(a).wait_recv()
                core_last(a).start()

        @pl.when(i >= LAG_OUT)
        def _():
            project(i - LAG_OUT)

        @pl.when((i >= LAG_MID) & (i < steps + LAG_MID))
        def _():
            bend(i - LAG_MID)

        @pl.when(i == 0)
        def _():
            for copy in weights:
                copy.wait_recv()

        @pl.when(i < last)
        def _():
            for a in range(2):
                core_copy(i, a).wait_recv()

        @pl.when(i == last)
        def _():
            for a in range(2):
                core_last(a).wait_recv()

        @pl.when(i < steps)
        def _():
            multiply(i)

    def chunk_of(q):
        where = (1 - core) if q == 0 else core
        return where * share

    def back_copy(t, q):
        chunk = pl.ds(pl.multiple_of(chunk_of(q), share), share)
        return remote(ring_out.at[t, chunk], ring_in.at[t - 1, chunk], back_send.at[t, q], back_recv.at[t, q], behind)

    def back_final(q):
        chunk = pl.ds(pl.multiple_of(chunk_of(q), share), share)
        return remote(ring_out.at[0, chunk], last_in.at[chunk], back_send.at[0, q], back_recv.at[0, q], behind)

    part_last().wait_recv()
    total = parts[last, far].astype(jnp.float32) + cross[last, pl.ds(0, share)].astype(jnp.float32)
    ring_out[last, here] = total.astype(jnp.bfloat16)
    back_copy(last, 1).start()

    @pl.loop(0, last)
    def _(i):
        t = last - 1 - i
        part_copy(t).wait_recv()
        for q in range(2):
            chunk = pl.ds(pl.multiple_of(chunk_of(q), share), share)
            source = pl.ds(pl.multiple_of(core * block + chunk_of(q), share), share)
            if q == 0:
                @pl.when(i > 0)
                def _():
                    back_copy(t + 1, 0).wait_recv()
            else:
                back_copy(t + 1, 1).wait_recv()
            total = parts[t, source].astype(jnp.float32) + cross[t, chunk].astype(jnp.float32)
            ring_out[t, chunk] = (total + ring_in[t, chunk].astype(jnp.float32)).astype(jnp.bfloat16)

            @pl.when(t > 0)
            def _():
                back_copy(t, q).start()

            @pl.when(t == 0)
            def _():
                back_final(q).start()

    there = part_of(1 - core, share)
    final = remote(last_total, last_cross, last_send.at[0], last_recv.at[0], twin)
    back_final(0).wait_recv()
    last_total[...] = (
        parts[last, there].astype(jnp.float32) + last_in[there].astype(jnp.float32)
    ).astype(jnp.bfloat16)
    final.start()
    back_final(1).wait_recv()
    total = parts[last, here].astype(jnp.float32) + last_in[here].astype(jnp.float32)
    final.wait_recv()
    final_rows[...] = (total + last_cross[...].astype(jnp.float32)).astype(jnp.bfloat16)

    def return_copy(d):
        to = lax.rem(grp + d, groups)
        return remote(
            final_rows.at[part_of(to, MOST)], returned.at[part_of(expert, MOST), mine],
            return_send.at[to], return_recv.at[grp], (to, frm),
        )

    def return_arrival(d):
        to = lax.rem(grp + d, groups)
        return remote(
            final_rows.at[part_of(to, MOST)],
            returned.at[part_of(lax.div(to, 2), MOST), part_of(lax.rem(to, 2), half)],
            return_send.at[to], return_recv.at[to], (to, frm),
        )

    return_own = pltpu.make_async_copy(
        final_rows.at[part_of(grp, MOST)], returned.at[part_of(expert, MOST), mine], return_send.at[grp]
    )

    @pl.loop(1, groups)
    def _(d):
        return_copy(d).start()

    return_own.start()

    @pl.loop(1, columns)
    def _(d):
        cot_copy(lax.rem(frm + d, columns)).wait_send()

    @pl.loop(1, groups)
    def _(d):
        for a in range(2):
            pick_copy(a, d).wait_send()

    for a in range(2):
        weights[a].wait_send()
        first(a).wait_send()
        ring_first(a).wait_send()
        ring_last(a).wait_send()
        core_last(a).wait_send()
        back_final(a).wait_send()
    part_last().wait_send()
    back_copy(last, 1).wait_send()
    final.wait_send()

    @pl.loop(0, steps)
    def _(t):
        x_copy(t).wait_send()
        slope_copy(t).wait_send()

        @pl.when(t < last)
        def _():
            part_copy(t).wait_send()
            for a in range(2):
                core_copy(t, a).wait_send()

        @pl.when((t > 0) & (t < last))
        def _():
            for a in range(2):
                ring(t, a).wait_send()
                back_copy(t, a).wait_send()

    return_own.wait()

    @pl.loop(1, groups)
    def _(d):
        return_copy(d).wait_send()
        return_arrival(d).wait_recv()

    back_ref[...] = returned[...]


def layer(query_in, key_in, value_in, cotangent, w_in, w_out, gates, chosen):
    levels = lax.axis_size("frm") // 2
    groups = lax.axis_size("grp")
    frames, blocks, features = query_in.shape
    local_rows = frames * blocks
    steps = levels // 2
    share = MOST * groups
    half = features // 2
    block = 2 * share
    hidden = w_in.shape[1]
    slots = MOST * chosen.shape[0]
    patches = blocks * groups * 2 * levels
    bf16 = jnp.bfloat16
    dma = pltpu.SemaphoreType.DMA
    vmem = pl.BlockSpec(memory_space=pltpu.VMEM)
    hbm = pl.BlockSpec(memory_space=pl.ANY)
    return pl.pallas_call(
        functools.partial(layer_kernel, levels, groups, patches),
        out_shape=(
            jax.ShapeDtypeStruct((HEADS, local_rows, local_rows), jnp.float32),
            jax.ShapeDtypeStruct((slots, local_rows), bf16),
            jax.ShapeDtypeStruct((local_rows, features), bf16),
            jax.ShapeDtypeStruct((slots, features), bf16),
        ),
        in_specs=[hbm] * 6 + [vmem] * 2,
        out_specs=(vmem,) * 4,
        scratch_shapes=[
            pltpu.VMEM((local_rows, features), bf16),
            pltpu.VMEM((local_rows, features), bf16),
            pltpu.VMEM((local_rows, features), bf16),
            pltpu.VMEM((local_rows, features), bf16),
            pltpu.VMEM((local_rows, features), bf16),
            pltpu.VMEM((2, slots, features), bf16),
            pltpu.VMEM((slots, features), bf16),
            pltpu.VMEM((share, half), bf16),
            pltpu.VMEM((2, steps, 2 * block, half), bf16),
            pltpu.VMEM((half, 2 * hidden), bf16),
            pltpu.VMEM((2 * hidden, half), bf16),
            pltpu.VMEM((steps, 2, 2 * block, hidden), jnp.float32),
            pltpu.VMEM((steps, 2, 2 * block, hidden), bf16),
            pltpu.VMEM((steps, 2, 2 * block, hidden), bf16),
            pltpu.VMEM((steps, 2 * block, 2 * hidden), bf16),
            pltpu.VMEM((steps, 2 * block, half), bf16),
            pltpu.VMEM((steps, block, half), bf16),
            pltpu.VMEM((steps, block, half), bf16),
            pltpu.VMEM((steps, block, half), bf16),
            pltpu.VMEM((block, half), bf16),
            pltpu.VMEM((share, half), bf16),
            pltpu.VMEM((share, half), bf16),
            dma((3,)), dma((3,)), dma((2,)), dma((2,)), dma((2,)), dma((2,)),
            dma((steps, 2)), dma((steps, 2)), dma((steps, 2)), dma((steps, 2)),
            dma((steps,)), dma((steps,)), dma((steps,)), dma((steps,)),
            dma((steps,)), dma((steps,)), dma((steps, 2)), dma((steps, 2)), dma((1,)), dma((1,)),
            dma((2 * levels,)), dma((2 * levels,)), dma((2, groups)), dma((2, groups)),
            dma((groups,)), dma((groups,)),
        ],
        compiler_params=pltpu.CompilerParams(
            collective_id=0, has_side_effects=True, vmem_limit_bytes=48 * 1024 * 1024
        ),
        name="layer",
    )(query_in, key_in, value_in, cotangent, w_in, w_out, gates, chosen)


def attention_kernel(
    query_ref, key_ref, value_ref, probs_ref, onehot_ref, stream_ref, back_ref,
    grad_query_ref, grad_key_ref, grad_value_ref,
):
    frames, blocks, width = query_ref.shape
    local_rows = frames * blocks
    heads = probs_ref.shape[0]
    head_dim = width // heads
    scaling = head_dim ** (-0.5)
    added = lax.dot_general(
        onehot_ref[...], back_ref[...], TN_DIMS, preferred_element_type=jnp.float32
    )
    stream = (stream_ref[...].astype(jnp.float32) + added).astype(jnp.bfloat16)
    for n in range(heads):
        cols = slice(n * head_dim, (n + 1) * head_dim)
        grad = stream[:, cols]
        query = query_ref[:, :, cols].reshape(local_rows, head_dim)
        key = key_ref[:, :, cols].reshape(local_rows, head_dim)
        value = value_ref[:, :, cols].reshape(local_rows, head_dim)
        probs = probs_ref[n]
        grad_value = lax.dot_general(
            probs.astype(jnp.bfloat16), grad, TN_DIMS, preferred_element_type=jnp.float32
        )
        grad_value_ref[:, :, cols] = grad_value.astype(jnp.bfloat16).reshape(frames, blocks, head_dim)
        grad_prob = lax.dot_general(grad, value, NT_DIMS, preferred_element_type=jnp.float32)
        centre = jnp.sum(probs * grad_prob, axis=1, keepdims=True)
        grad_score = (probs * (grad_prob - centre)).astype(jnp.bfloat16)
        grad_query = jnp.dot(grad_score, key, preferred_element_type=jnp.float32) * scaling
        grad_query_ref[:, :, cols] = grad_query.astype(jnp.bfloat16).reshape(frames, blocks, head_dim)
        grad_key = lax.dot_general(grad_score, query, TN_DIMS, preferred_element_type=jnp.float32) * scaling
        grad_key_ref[:, :, cols] = grad_key.astype(jnp.bfloat16).reshape(frames, blocks, head_dim)


def attention_back(query_in, key_in, value_in, probs, onehot, stream, back):
    frames, blocks, features = query_in.shape
    local_rows = frames * blocks
    slots = onehot.shape[0]
    pieces = 4
    width = features // pieces
    whole = pl.BlockSpec((frames, blocks, width), lambda n: (0, 0, n))
    return pl.pallas_call(
        attention_kernel,
        grid=(pieces,),
        out_shape=(jax.ShapeDtypeStruct(query_in.shape, jnp.bfloat16),) * 3,
        in_specs=[
            whole, whole, whole,
            pl.BlockSpec((HEADS // pieces, local_rows, local_rows), lambda n: (n, 0, 0)),
            pl.BlockSpec((slots, local_rows), lambda n: (0, 0)),
            pl.BlockSpec((local_rows, width), lambda n: (0, n)),
            pl.BlockSpec((slots, width), lambda n: (0, n)),
        ],
        out_specs=(whole,) * 3,
        compiler_params=pltpu.CompilerParams(dimension_semantics=("arbitrary",)),
        name="attention_back",
    )(query_in, key_in, value_in, probs, onehot, stream, back)


def body(query_in, key_in, value_in, cotangent, w_in, w_out, gate_probs, chosen):
    probs, onehot, stream, back = layer(
        query_in, key_in, value_in, cotangent, w_in[0], w_out[0], gate_probs, chosen
    )
    return attention_back(query_in, key_in, value_in, probs, onehot, stream, back)


def solution(mesh):
    return jax.shard_map(
        body,
        mesh=mesh,
        in_specs=(
            P(None, ("grp", "frm"), None),
            P(None, ("grp", "frm"), None),
            P(None, ("grp", "frm"), None),
            P("frm", "grp", None),
            P("grp", None, "frm"),
            P("grp", "frm", None),
            P(),
            P(),
        ),
        out_specs=(
            P(None, ("grp", "frm"), None),
            P(None, ("grp", "frm"), None),
            P(None, ("grp", "frm"), None),
        ),
        check_vma=False,
    )
```

time: 169 us -> 143 us (0.85)
  Pallas kernels: 76.5 us -> 132 us
  waiting for transfers between devices: 30.4 us -> 0 us
  starting transfers between devices: 21.2 us -> 0 us
  blocking collectives: 13.2 us -> 0 us
  other arithmetic: 5.65 us -> 0 us
  matrix products: 4.98 us -> 0 us
  local copies, waits for them, and re-layouts: 15.3 us -> 10.7 us
    pallas_call x1 -> x2, Pallas kernels: 76.5 us -> 132 us  [the longest x1 124 us: layer(): pl.pallas_call(functools.partial(layer_kernel, levels, groups, patches),...]
    all_to_all x2 -> x0, waiting for transfers between devices: 30.4 us -> none  [the longest x1 25.1 us: body(): lax.all_to_all(cotangent, 'frm', split_axis=1, concat_axis=0, tiled=True)]
    all_to_all x2 -> x0, starting transfers between devices: 21.2 us -> none  [the longest x1 15.6 us: body(): lax.all_to_all(cotangent, 'frm', split_axis=1, concat_axis=0, tiled=True)]
    all_to_all x1 -> x0, blocking collectives: 13.2 us -> none  [body(): lax.all_to_all(outgoing, 'grp', split_axis=0, concat_axis=0, tiled=True)]
    dot_general x8 -> x0, matrix products: 4.03 us -> none  [the longest x1 0.86 us: body(): jnp.einsum('fphd,gphd->phfg', grad_heads, value_heads, preferred_element_...]
    unnamed x1 -> x0, other arithmetic: 3.7 us -> none
    reshape x6 -> x0, local copies, waits for them, and re-layouts: 1.93 us -> none  [the longest x1 0.66 us: body(): summed.reshape(groups, MOST, half)]
    unnamed x36 -> x24, local copies, waits for them, and re-layouts: 11.7 us -> 10.7 us
  transfers between devices with their start and end apart: 2 -> 0, of which waited for: 2 -> 0; matrix products, arithmetic and copies ran while one was open for 3% -> 0% of each run, Pallas kernels for 0% -> 0%
where the time goes in v2:
time: 143 us
  Pallas kernels  132 us (92%)
  local copies, waits for them, and re-layouts  10.7 us (7%)
    pallas_call x1, Pallas kernels, layer(): pl.pallas_call(functools.partial(layer_kernel, levels, groups, patches),...  124 us
    unnamed x24, local copies, waits for them, and re-layouts  10.7 us
    pallas_call x1, Pallas kernels, attention_back(): pl.pallas_call(attention_kernel, grid=(pieces,), out_shape=(jax.ShapeDtyp...  7.76 us

profile of v2, /device:TPU:6, one launch (start us, length us, event | category | flops | bytes accessed | tf_op | source)
XLA Modules:
  0.0 142.9 jit_solution(17386590216192269005)
XLA Ops:
  0.6 0.0 copy-start
  0.6 1.0 copy-done
  1.7 0.0 copy-start.1
  1.7 1.0 copy-done.1
  2.7 0.0 copy-start.2
  2.7 1.0 copy-done.2
  3.8 0.0 copy-start.4
  3.8 1.0 copy-done.4
  4.8 0.0 copy-start.5
  4.8 1.0 copy-done.5
  5.8 0.0 copy-start.6
  5.8 1.0 copy-done.6
  6.9 0.0 copy-start.9
  6.9 0.7 copy-done.9
  7.6 0.0 copy-start.10
  7.6 0.7 copy-done.10
  8.3 123.8 %layer.1 = (f32[16,128,128]{2,1,0:T(8,128)S(1)}, bf16[16,128]{1,0:T(8,128)(2,1)S(1)}, bf16[128,2048]{1,0:T(8,128)(2,1)S(1)}, bf16[16,2048]{1,0:T(8,128)(2,1)S(1)}) custom-call(bf16[32,4,2048]{2,1,0:T(4,128)(2,1)S(1)} %copy-done, bf16[32,4,2048]{2,1,0:T(4,128)(2,1)S(1)} %copy-done.1, bf16[32,4,2048]{2,1,0:T(4,128)(2,1)S(1)} %copy-done.2, ...), custom_call_target="tpu_custom_call" | custom-call | tf_op jit(solution)/shard_map/layer/pallas_call | solution.py:535
  132.2 0.0 copy-start.3
  132.2 1.0 copy-done.3
  133.2 0.0 copy-start.7
  133.2 0.8 copy-done.7
  134.0 0.0 copy-start.8
  134.0 0.6 copy-done.8
  134.6 0.0 copy-start.11
  134.6 0.6 copy-done.11
  135.2 7.8 %attention_back.1 = (bf16[32,4,2048]{2,1,0:T(4,128)(2,1)}, bf16[32,4,2048]{2,1,0:T(4,128)(2,1)}, bf16[32,4,2048]{2,1,0:T(4,128)(2,1)}) custom-call(bf16[32,4,2048]{2,1,0:T(4,128)(2,1)} %query_ref.3, bf16[32,4,2048]{2,1,0:T(4,128)(2,1)} %key_ref.3, bf16[32,4,2048]{2,1,0:T(4,128)(2,1)} %value_ref.3, f32[16,128,128]{2,1,0:T(8,128)} %copy-done.3, ...), custom_call_target="tpu_custom_call" | custom-call | tf_op jit(solution)/shard_map/attention_back/pallas_call | solution.py:622
Async XLA Ops:
  0.6 1.0 copy-start
  1.7 1.0 copy-start.1
  2.7 1.0 copy-start.2
  3.8 1.0 copy-start.4
  4.8 1.0 copy-start.5
  5.8 1.0 copy-start.6
  6.9 0.7 copy-start.9
  7.6 0.7 copy-start.10
  132.2 1.0 copy-start.3
  133.2 0.8 copy-start.7
  134.0 0.6 copy-start.8
  134.6 0.6 copy-start.11

commit v3 on v2

v3 whole, which is shorter than its diff:
```python
import functools

import jax
import jax.numpy as jnp
from jax import lax
from jax.experimental import pallas as pl
from jax.experimental.pallas import tpu as pltpu
from jax.sharding import PartitionSpec as P

HEADS = 16
MOST = 2
MESH = pl.DeviceIdType.MESH

root_half = 0.7071067811865476
inv_root_tau = 0.3989422804014327


def gelu_slope(pre_act):
    normal_cdf = 0.5 * (1.0 + lax.erf(pre_act * root_half))
    density = jnp.exp(-0.5 * pre_act * pre_act) * inv_root_tau
    return normal_cdf + pre_act * density


NT_DIMS = (((1,), (1,)), ((), ()))
TN_DIMS = (((0,), (0,)), ((), ()))
LAG_MID = 2
LAG_OUT = 4
LEAD = 1
PIECES = 2
CHUNKS = 4
WIDE = 4


def bits(n):
    assert n & (n - 1) == 0
    return n.bit_length() - 1


def onehot_rows(chosen, gates, myself, blocks, patches, local_rows):
    experts_total, cap = chosen.shape
    slots = MOST * experts_total

    def twice(values):
        spread = jnp.broadcast_to(values[:, None, :], (experts_total, MOST, cap))
        return spread.reshape(slots, cap)

    token = twice(chosen)
    gate = twice(gates)
    patch = token & (patches - 1)
    frame = lax.shift_right_logical(token, bits(patches))
    holder = lax.shift_right_logical(patch, bits(blocks))
    place = frame * blocks + (patch & (blocks - 1))
    order = lax.broadcasted_iota(jnp.int32, (slots, cap), 1)
    key = (order * local_rows + place).astype(jnp.float32)
    owned = holder == myself
    beyond = float(cap * local_rows)
    low = jnp.min(jnp.where(owned, key, beyond), axis=1, keepdims=True)
    high = jnp.max(jnp.where(owned, key, -1.0), axis=1, keepdims=True)
    odd = (lax.broadcasted_iota(jnp.int32, (slots, 1), 0) & 1) == 1
    key_at = jnp.where(odd, high, low)
    present = jnp.where(odd, (high > low).astype(jnp.float32), (low < beyond).astype(jnp.float32))
    place_at = key_at - jnp.floor(key_at * (1.0 / local_rows)) * local_rows
    gate_at = jnp.sum(jnp.where(owned & (key == key_at), gate, 0.0), axis=1, keepdims=True)
    row = lax.broadcasted_iota(jnp.int32, (slots, local_rows), 1).astype(jnp.float32)
    hit = jnp.where((row == place_at) & (present > 0.5), 1.0, 0.0)
    return hit.astype(jnp.bfloat16), gate_at


def layer_kernel(
    levels, groups, patches,
    query_ref, key_ref, value_ref, cot_ref, w_in_ref, w_out_ref, gates_ref, chosen_ref,
    probs_ref, onehot_ref, stream_ref, query_rows_ref, key_rows_ref, value_rows_ref, back_ref,
    query, key, value, mixed, cot_rows, probs_all, onehot_all, picked, returned, final_rows,
    gathered, w1, w2, own, x_send, x_recv, slopes, parts, cross, ring_in, ring_out,
    last_in, gauge,
    local_sem, load_sem, out_sem, own_sem, weight_send, weight_recv,
    ring_send, ring_recv, core_send, core_recv, x_send_sem, x_recv_sem,
    slope_send, slope_recv, part_send, part_recv, back_send, back_recv, last_recv,
    cot_send, cot_recv, pick_send, pick_recv, return_send, return_recv,
):
    steps = levels // 2
    last = steps - 1
    columns = 2 * levels
    frames, blocks, features = query_ref.shape
    local_rows = frames * blocks
    head_dim = features // HEADS
    half = features // 2
    share = MOST * groups
    block = 2 * share
    hidden = w_in_ref.shape[1]
    grp = lax.axis_index("grp")
    frm = lax.axis_index("frm")
    side = lax.rem(grp, 2)
    expert = lax.div(grp, 2)
    core = lax.rem(frm, 2)
    level = lax.div(frm, 2)
    turn = 1 - 2 * core
    ahead = (grp, lax.rem(level + turn + levels, levels) * 2 + core)
    behind = (grp, lax.rem(level - turn + levels, levels) * 2 + core)
    twin = (grp, frm + turn)
    mate = (grp + 1 - 2 * side, frm)

    def remote(src, dst, send, recv, device):
        return pltpu.make_async_remote_copy(
            src_ref=src, dst_ref=dst, send_sem=send, recv_sem=recv, device_id=device, device_id_type=MESH
        )

    def bulk(elements, send, recv):
        lines = elements // (2 * gauge.shape[2])
        many = max(n for n in range(1, gauge.shape[0] + 1) if lines % (8 * n) == 0)
        assert lines * 2 * gauge.shape[2] == elements and lines // many <= gauge.shape[1]
        ref = gauge.at[pl.ds(0, many), pl.ds(0, lines // many)]
        return remote(ref, ref, send, recv, twin)

    def part_of(index, size):
        return pl.ds(pl.multiple_of(index * size, size), size)

    barrier = pltpu.get_barrier_semaphore()

    @pl.loop(1, columns)
    def _(d):
        pl.semaphore_signal(
            barrier, inc=1, device_id=(grp, lax.rem(frm + d, columns)), device_id_type=MESH
        )

    @pl.loop(1, groups)
    def _(d):
        for k in range(2):
            pl.semaphore_signal(
                barrier, inc=1, device_id=(lax.rem(grp + d, groups), frm + k * turn), device_id_type=MESH
            )

    mine = part_of(side, half)
    theirs = part_of(1 - side, half)
    here = part_of(core, share)
    there = part_of(1 - core, share)
    lane = part_of(core, block)
    other_lane = part_of(1 - core, block)
    lane_part = pl.ds(pl.multiple_of(core * (block + share), share), share)
    far = pl.ds(pl.multiple_of(block + core * share, share), share)
    other_far = pl.ds(pl.multiple_of(block + (1 - core) * share, share), share)

    ring_in[last - 1] = jnp.zeros(ring_in.shape[1:], ring_in.dtype)
    pl.semaphore_wait(barrier, columns - 1 + 2 * (groups - 1))

    def cot_copy(other):
        return remote(
            cot_ref.at[0, part_of(other, blocks)], cot_rows.at[part_of(frm, blocks)],
            cot_send.at[0], cot_recv.at[0], (grp, other),
        )

    def cot_all():
        return bulk((columns - 1) * blocks * features, cot_send.at[0], cot_recv.at[0])

    @pl.loop(0, levels - 1)
    def _(k):
        away = steps - lax.div(k + 1, 2)
        to = lax.rem(level + levels + (2 * lax.rem(k, 2) - 1) * away, levels)
        cot_copy(2 * to + core).start()
        cot_copy(2 * to + 1 - core).start()

    cot_copy(frm + turn).start()
    weights = [
        remote(w_in_ref.at[theirs], w1.at[:, pl.ds(hidden, hidden)], weight_send.at[0], weight_recv.at[0], mate),
        remote(w_out_ref.at[:, theirs], w2.at[pl.ds(hidden, hidden)], weight_send.at[0], weight_recv.at[0], mate),
    ]
    for copy in weights:
        copy.start()

    def weights_all():
        return remote(w1, w1, weight_send.at[0], weight_recv.at[0], mate)


    inputs = ((query_ref, query), (key_ref, key), (value_ref, value))

    @pl.loop(0, frames)
    def _(f):
        for n, (src, dst) in enumerate(inputs):
            pltpu.make_async_copy(src.at[f], dst.at[part_of(f, blocks)], load_sem.at[n]).start()

    local = [
        pltpu.make_async_copy(w_in_ref.at[mine], w1.at[:, pl.ds(0, hidden)], local_sem.at[0]),
        pltpu.make_async_copy(w_out_ref.at[:, mine], w2.at[pl.ds(0, hidden)], local_sem.at[1]),
        pltpu.make_async_copy(
            cot_ref.at[0, part_of(frm, blocks)], cot_rows.at[part_of(frm, blocks)], local_sem.at[2]
        ),
    ]
    for copy in local:
        copy.start()
    myself = grp * columns + frm
    onehot, gate_at = onehot_rows(chosen_ref[...], gates_ref[...], myself, blocks, patches, local_rows)
    onehot_all[...] = onehot

    for n, (_, dst) in enumerate(inputs):
        pltpu.make_async_copy(dst, dst, load_sem.at[n]).wait()
    row_patch = lax.broadcasted_iota(jnp.int32, (local_rows, local_rows), 0) & (blocks - 1)
    column_patch = lax.broadcasted_iota(jnp.int32, (local_rows, local_rows), 1) & (blocks - 1)
    same = row_patch == column_patch
    scaling = head_dim ** (-0.5)
    together = 4

    @pl.loop(0, HEADS // together)
    def _(n):
        for m in range(together):
            head = n * together + m
            cols = part_of(head, head_dim)
            scores = lax.dot_general(
                query[:, cols], key[:, cols], NT_DIMS, preferred_element_type=jnp.float32
            ) * scaling
            scores = jnp.where(same, scores, -1e30)
            raised = jnp.exp(scores - jnp.max(scores, axis=1, keepdims=True))
            probs = raised / jnp.sum(raised, axis=1, keepdims=True)
            probs_all[head] = probs
            mixed[:, cols] = jnp.dot(
                probs.astype(jnp.bfloat16), value[:, cols], preferred_element_type=jnp.float32
            ).astype(jnp.bfloat16)

    outs = [
        pltpu.make_async_copy(src, dst, out_sem.at[n])
        for n, (src, dst) in enumerate((
            (probs_all, probs_ref), (onehot_all, onehot_ref), (query, query_rows_ref),
            (key, key_rows_ref), (value, value_rows_ref), (cot_rows, stream_ref),
        ))
    ]

    def pick_copy(a, d, k):
        to = lax.rem(grp + d, groups)
        return remote(
            picked.at[a, part_of(lax.div(to, 2), MOST), part_of(lax.rem(to, 2), half)],
            gathered.at[a, last, pl.ds(pl.multiple_of(core * share + grp * MOST, MOST), MOST)],
            pick_send.at[a], pick_recv.at[a], (to, frm + k * turn),
        )

    def pick_all(a):
        return bulk((block - MOST) * half, pick_send.at[a], pick_recv.at[a])

    def pick_own(a):
        return pltpu.make_async_copy(
            picked.at[a, part_of(expert, MOST), part_of(side, half)],
            gathered.at[a, last, pl.ds(pl.multiple_of(core * share + grp * MOST, MOST), MOST)],
            own_sem.at[a],
        )

    def send_picked(a):
        @pl.loop(1, groups)
        def _(d):
            for k in range(2):
                pick_copy(a, d, k).start()

        pick_copy(a, 0, 1).start()
        pick_own(a).start()

    def take_picked(a):
        pick_own(a).wait()
        pick_all(a).wait_recv()
        for k in range(PIECES):
            ring_first(a, k).start()

    picked[0] = jnp.dot(onehot, mixed[...], preferred_element_type=jnp.float32).astype(jnp.bfloat16)
    send_picked(0)
    for copy in outs[:5]:
        copy.start()

    slab = block // PIECES

    def lane_slab(k):
        return pl.ds(pl.multiple_of(core * block + k * slab, slab), slab)

    def ring(t, a, k):
        return remote(
            gathered.at[a, lax.max(t - 1, 0), lane_slab(k)], gathered.at[a, t, lane_slab(k)],
            ring_send.at[0], ring_recv.at[t, a, k], ahead,
        )

    def ring_first(a, k):
        return remote(
            gathered.at[a, last, pl.ds(k * slab, slab)], gathered.at[a, 0, lane_slab(k)],
            ring_send.at[0], ring_recv.at[0, a, k], ahead,
        )

    def ring_last(a):
        return remote(
            gathered.at[a, last - 1, lane_part], gathered.at[a, last, far],
            ring_send.at[0], ring_recv.at[last, a, 0], ahead,
        )

    def core_copy(t, a, k):
        return remote(
            gathered.at[a, t, lane_slab(k)], gathered.at[a, t, lane_slab(k)],
            core_send.at[0], core_recv.at[t], twin,
        )

    def core_last(a):
        return remote(
            gathered.at[a, last, far], gathered.at[a, last, far],
            core_send.at[0], core_recv.at[last], twin,
        )

    def advance(t, a, k):
        @pl.when(t < last)
        def _():
            ring(t, a, k).wait_recv()

            @pl.when(t < last - 1)
            def _():
                ring(t + 1, a, k).start()

            if k == PIECES - 1:
                @pl.when(t == last - 1)
                def _():
                    ring_last(a).start()

            core_copy(t, a, k).start()

        if k == 0:
            @pl.when(t == last)
            def _():
                ring_last(a).wait_recv()
                core_last(a).start()

    def x_copy(t):
        return remote(x_send.at[t], x_recv.at[t], x_send_sem.at[0], x_recv_sem.at[t], mate)

    def slope_copy(t):
        return remote(
            slopes.at[t, :, pl.ds(0, hidden)], slopes.at[t, :, pl.ds(hidden, hidden)],
            slope_send.at[0], slope_recv.at[t], mate,
        )

    def part_copy(t):
        return remote(parts.at[t, other_lane], cross.at[t], part_send.at[0], part_recv.at[t], twin)

    def part_own():
        return remote(
            parts.at[last, there], cross.at[last, pl.ds(share, share)],
            part_send.at[0], part_recv.at[steps], twin,
        )

    def part_last():
        return remote(
            parts.at[last, other_far], cross.at[last, pl.ds(0, share)],
            part_send.at[0], part_recv.at[last], twin,
        )

    take_picked(0)
    local[2].wait()

    cot_all().wait_recv()

    picked_cot = jnp.dot(onehot_all[...], cot_rows[...], preferred_element_type=jnp.float32)
    picked[1] = (gate_at * picked_cot).astype(jnp.bfloat16)
    send_picked(1)
    for n in range(LEAD):
        for k in range(PIECES):
            advance(jnp.int32(n), 0, k)
    outs[5].start()
    for copy in local[:2]:
        copy.wait()
    take_picked(1)

    def multiply(t):
        pre = jnp.dot(gathered[0, t], w1[...], preferred_element_type=jnp.float32)
        own[t, 0] = pre[:, :hidden]
        x_send[t, 0] = pre[:, hidden:].astype(jnp.bfloat16)
        back = lax.dot_general(gathered[1, t], w2[...], NT_DIMS, preferred_element_type=jnp.float32)
        own[t, 1] = back[:, :hidden]
        x_send[t, 1] = back[:, hidden:].astype(jnp.bfloat16)
        x_copy(t).start()

    def bend(t):
        x_copy(t).wait_recv()
        pre = own[t, 0] + x_recv[t, 0].astype(jnp.float32)
        back = own[t, 1] + x_recv[t, 1].astype(jnp.float32)
        slopes[t, :, pl.ds(0, hidden)] = (back * gelu_slope(pre)).astype(jnp.bfloat16)
        slope_copy(t).start()

    def project(t):
        slope_copy(t).wait_recv()
        parts[t] = lax.dot_general(
            slopes[t], w1[...], NT_DIMS, preferred_element_type=jnp.float32
        ).astype(jnp.bfloat16)

        @pl.when(t < last)
        def _():
            part_copy(t).start()

        @pl.when(t == last)
        def _():
            part_last().start()
            part_own().start()

    @pl.loop(0, steps + LAG_OUT)
    def _(i):
        for k in range(PIECES):
            advance(i, 1, k)
            advance(i + LEAD, 0, k)

        @pl.when((i >= LAG_MID) & (i < steps + LAG_MID))
        def _():
            bend(i - LAG_MID)

        @pl.when(i >= LAG_OUT)
        def _():
            project(i - LAG_OUT)

        @pl.when(i == 0)
        def _():
            weights_all().wait_recv()

        @pl.when(i < last)
        def _():
            whole = gathered.at[:, i, other_lane]
            remote(whole, whole, core_send.at[0], core_recv.at[i], twin).wait_recv()

        @pl.when(i == last)
        def _():
            whole = gathered.at[:, last, other_far]
            remote(whole, whole, core_send.at[0], core_recv.at[last], twin).wait_recv()

        @pl.when(i < steps)
        def _():
            multiply(i)

    piece = block // CHUNKS

    def chunk_of(q):
        where = (1 - core) if q < CHUNKS // 2 else core
        return where * share + (q % (CHUNKS // 2)) * piece

    def back_copy(t, q):
        chunk = pl.ds(pl.multiple_of(chunk_of(q), piece), piece)
        return remote(
            ring_out.at[t, chunk], ring_in.at[lax.max(t - 1, 0), chunk], back_send.at[0], back_recv.at[t, q], behind
        )

    def back_final(q):
        chunk = pl.ds(pl.multiple_of(chunk_of(q), piece), piece)
        n = q % (CHUNKS // 2)
        owner = (1 - core) if q < CHUNKS // 2 else core
        return remote(
            ring_out.at[0, chunk], last_in.at[core, pl.ds(n * piece, piece)],
            back_send.at[0], last_recv.at[core, n], (grp, behind[1] - core + owner),
        )

    def back_arrival(way, n):
        return remote(
            ring_out.at[0, pl.ds(0, piece)], last_in.at[way, pl.ds(n * piece, piece)],
            back_send.at[0], last_recv.at[way, n], ahead,
        )

    part_last().wait_recv()
    for q in range(CHUNKS // 2, CHUNKS):
        chunk = pl.ds(pl.multiple_of(chunk_of(q), piece), piece)
        source = pl.ds(pl.multiple_of(block + chunk_of(q), piece), piece)
        other = pl.ds((q - CHUNKS // 2) * piece, piece)
        total = parts[last, source].astype(jnp.float32) + cross[last, other].astype(jnp.float32)
        ring_out[last, chunk] = total.astype(jnp.bfloat16)
        back_copy(last, q).start()

    @pl.loop(0, last)
    def _(i):
        t = last - 1 - i
        part_copy(t).wait_recv()
        for q in range(CHUNKS):
            chunk = pl.ds(pl.multiple_of(chunk_of(q), piece), piece)
            source = pl.ds(pl.multiple_of(core * block + chunk_of(q), piece), piece)
            total = parts[t, source].astype(jnp.float32) + cross[t, chunk].astype(jnp.float32)
            if q < CHUNKS // 2:
                @pl.when(i > 0)
                def _():
                    back_copy(t + 1, q).wait_recv()
            else:
                back_copy(t + 1, q).wait_recv()
            ring_out[t, chunk] = (total + ring_in[t, chunk].astype(jnp.float32)).astype(jnp.bfloat16)

            @pl.when(t > 0)
            def _():
                back_copy(t, q).start()

            @pl.when(t == 0)
            def _():
                back_final(q).start()

    def return_copy(to):
        return remote(
            final_rows.at[part_of(to, MOST)], returned.at[part_of(expert, MOST), mine],
            return_send.at[0], return_recv.at[0], (to, frm),
        )

    def return_all():
        return bulk((share - MOST) * half, return_send.at[0], return_recv.at[0])

    return_own = pltpu.make_async_copy(
        final_rows.at[part_of(grp, MOST)], returned.at[part_of(expert, MOST), mine], own_sem.at[2]
    )
    part_own().wait_recv()
    reach = piece // MOST
    for n in range(CHUNKS // 2):
        rows = pl.ds(pl.multiple_of(core * share + n * piece, piece), piece)
        other = pl.ds(share + n * piece, piece)
        chunk = pl.ds(n * piece, piece)
        total = parts[last, rows].astype(jnp.float32) + cross[last, other].astype(jnp.float32)
        for way in range(2):
            back_arrival(way, n).wait_recv()
        total = total + last_in[0, chunk].astype(jnp.float32) + last_in[1, chunk].astype(jnp.float32)
        final_rows[chunk] = total.astype(jnp.bfloat16)

        @pl.loop(0, reach)
        def _(j):
            to = n * reach + lax.rem(grp + j, reach)

            @pl.when(to != grp)
            def _():
                return_copy(to).start()

            @pl.when(to == grp)
            def _():
                return_own.start()

    cot_all().wait_send()

    for copy in outs:
        copy.wait()

    for a in range(2):
        pick_all(a).wait_send()
    weights_all().wait_send()
    moved = (last * block + share) * half
    bulk(2 * moved, ring_send.at[0], ring_recv.at[0, 0, 0]).wait_send()
    bulk(2 * moved, core_send.at[0], core_recv.at[0]).wait_send()
    remote(cross, cross, part_send.at[0], part_recv.at[0], twin).wait_send()
    remote(x_send, x_recv, x_send_sem.at[0], x_recv_sem.at[0], mate).wait_send()
    slopes_all = slopes.at[:, :, pl.ds(0, hidden)]
    remote(slopes_all, slopes_all, slope_send.at[0], slope_recv.at[0], mate).wait_send()
    bulk(moved, back_send.at[0], back_recv.at[0, 0]).wait_send()
    return_own.wait()

    return_all().wait_send()
    return_all().wait_recv()
    back_ref[...] = returned[...]


def layer(query_in, key_in, value_in, cotangent, w_in, w_out, gates, chosen):
    levels = lax.axis_size("frm") // 2
    groups = lax.axis_size("grp")
    frames, blocks, features = query_in.shape
    local_rows = frames * blocks
    steps = levels // 2
    share = MOST * groups
    half = features // 2
    block = 2 * share
    hidden = w_in.shape[1]
    slots = MOST * chosen.shape[0]
    patches = blocks * groups * 2 * levels
    bf16 = jnp.bfloat16
    dma = pltpu.SemaphoreType.DMA
    vmem = pl.BlockSpec(memory_space=pltpu.VMEM)
    hbm = pl.BlockSpec(memory_space=pl.ANY)
    return pl.pallas_call(
        functools.partial(layer_kernel, levels, groups, patches),
        out_shape=(
            jax.ShapeDtypeStruct((HEADS, local_rows, local_rows), jnp.float32),
            jax.ShapeDtypeStruct((slots, local_rows), bf16),
            jax.ShapeDtypeStruct((local_rows, features), bf16),
            jax.ShapeDtypeStruct((local_rows, features), bf16),
            jax.ShapeDtypeStruct((local_rows, features), bf16),
            jax.ShapeDtypeStruct((local_rows, features), bf16),
            jax.ShapeDtypeStruct((slots, features), bf16),
        ),
        in_specs=[hbm] * 6 + [vmem] * 2,
        out_specs=(hbm,) * 6 + (vmem,),
        scratch_shapes=[
            pltpu.VMEM((local_rows, features), bf16),
            pltpu.VMEM((local_rows, features), bf16),
            pltpu.VMEM((local_rows, features), bf16),
            pltpu.VMEM((local_rows, features), bf16),
            pltpu.VMEM((local_rows, features), bf16),
            pltpu.VMEM((HEADS, local_rows, local_rows), jnp.float32),
            pltpu.VMEM((slots, local_rows), bf16),
            pltpu.VMEM((2, slots, features), bf16),
            pltpu.VMEM((slots, features), bf16),
            pltpu.VMEM((share, half), bf16),
            pltpu.VMEM((2, steps, 2 * block, half), bf16),
            pltpu.VMEM((half, 2 * hidden), bf16),
            pltpu.VMEM((2 * hidden, half), bf16),
            pltpu.VMEM((steps, 2, 2 * block, hidden), jnp.float32),
            pltpu.VMEM((steps, 2, 2 * block, hidden), bf16),
            pltpu.VMEM((steps, 2, 2 * block, hidden), bf16),
            pltpu.VMEM((steps, 2 * block, 2 * hidden), bf16),
            pltpu.VMEM((steps, 2 * block, half), bf16),
            pltpu.VMEM((steps, block, half), bf16),
            pltpu.VMEM((steps, block, half), bf16),
            pltpu.VMEM((steps, block, half), bf16),
            pltpu.VMEM((2, share, half), bf16),
            pltpu.VMEM((32, 128, 128), jnp.float32),
            dma((3,)), dma((3,)), dma((6,)), dma((3,)), dma((1,)), dma((1,)),
            dma((1,)), dma((steps, 2, PIECES)), dma((1,)), dma((steps,)),
            dma((1,)), dma((steps,)), dma((1,)), dma((steps,)),
            dma((1,)), dma((steps + 1,)), dma((1,)), dma((steps, CHUNKS)), dma((2, CHUNKS // 2)),
            dma((1,)), dma((1,)), dma((2,)), dma((2,)), dma((1,)), dma((1,)),
        ],
        compiler_params=pltpu.CompilerParams(
            collective_id=0, has_side_effects=True
        ),
        name="layer",
    )(query_in, key_in, value_in, cotangent, w_in, w_out, gates, chosen)


def attention_kernel(
    query_ref, key_ref, value_ref, probs_ref, onehot_ref, stream_ref, back_ref,
    grad_query_ref, grad_key_ref, grad_value_ref,
):
    frames, blocks, width = grad_query_ref.shape
    local_rows = frames * blocks
    heads = probs_ref.shape[0]
    head_dim = width // heads
    scaling = head_dim ** (-0.5)
    added = lax.dot_general(
        onehot_ref[...], back_ref[...], TN_DIMS, preferred_element_type=jnp.float32
    )
    stream = (stream_ref[...].astype(jnp.float32) + added).astype(jnp.bfloat16)
    for n in range(heads):
        cols = slice(n * head_dim, (n + 1) * head_dim)
        grad = stream[:, cols]
        query = query_ref[:, cols]
        key = key_ref[:, cols]
        value = value_ref[:, cols]
        probs = probs_ref[n]
        grad_value = lax.dot_general(
            probs.astype(jnp.bfloat16), grad, TN_DIMS, preferred_element_type=jnp.float32
        )
        grad_value_ref[:, :, cols] = grad_value.astype(jnp.bfloat16).reshape(frames, blocks, head_dim)
        grad_prob = lax.dot_general(grad, value, NT_DIMS, preferred_element_type=jnp.float32)
        centre = jnp.sum(probs * grad_prob, axis=1, keepdims=True)
        grad_score = (probs * (grad_prob - centre)).astype(jnp.bfloat16)
        grad_query = jnp.dot(grad_score, key, preferred_element_type=jnp.float32) * scaling
        grad_query_ref[:, :, cols] = grad_query.astype(jnp.bfloat16).reshape(frames, blocks, head_dim)
        grad_key = lax.dot_general(grad_score, query, TN_DIMS, preferred_element_type=jnp.float32) * scaling
        grad_key_ref[:, :, cols] = grad_key.astype(jnp.bfloat16).reshape(frames, blocks, head_dim)


def attention_back(frames, query, key, value, probs, onehot, stream, back):
    local_rows, features = query.shape
    blocks = local_rows // frames
    slots = onehot.shape[0]
    width = features // WIDE
    rows = pl.BlockSpec((local_rows, width), lambda n: (0, n))
    whole = pl.BlockSpec((frames, blocks, width), lambda n: (0, 0, n))
    return pl.pallas_call(
        attention_kernel,
        grid=(WIDE,),
        out_shape=(jax.ShapeDtypeStruct((frames, blocks, features), jnp.bfloat16),) * 3,
        in_specs=[
            rows, rows, rows,
            pl.BlockSpec((HEADS // WIDE, local_rows, local_rows), lambda n: (n, 0, 0)),
            pl.BlockSpec((slots, local_rows), lambda n: (0, 0)),
            rows,
            pl.BlockSpec((slots, width), lambda n: (0, n)),
        ],
        out_specs=(whole,) * 3,
        compiler_params=pltpu.CompilerParams(dimension_semantics=("arbitrary",)),
        name="attention_back",
    )(query, key, value, probs, onehot, stream, back)


def body(query_in, key_in, value_in, cotangent, w_in, w_out, gate_probs, chosen):
    probs, onehot, stream, query, key, value, back = layer(
        query_in, key_in, value_in, cotangent, w_in[0], w_out[0], gate_probs, chosen
    )
    return attention_back(query_in.shape[0], query, key, value, probs, onehot, stream, back)


def solution(mesh):
    return jax.shard_map(
        body,
        mesh=mesh,
        in_specs=(
            P(None, ("grp", "frm"), None),
            P(None, ("grp", "frm"), None),
            P(None, ("grp", "frm"), None),
            P("frm", "grp", None),
            P("grp", None, "frm"),
            P("grp", "frm", None),
            P(),
            P(),
        ),
        out_specs=(
            P(None, ("grp", "frm"), None),
            P(None, ("grp", "frm"), None),
            P(None, ("grp", "frm"), None),
        ),
        check_vma=False,
    )
```

time: 143 us -> 125 us (0.87)
  local copies, waits for them, and re-layouts: 10.7 us -> 0 us
  Pallas kernels: 132 us -> 124 us
    unnamed x24 -> x0, local copies, waits for them, and re-layouts: 10.7 us -> none
    pallas_call x1, Pallas kernels: 124 us -> 116 us  [layer(): pl.pallas_call(functools.partial(layer_kernel, levels, groups, patches),...]
where the time goes in v3:
time: 125 us
  Pallas kernels  124 us (99%)
    pallas_call x1, Pallas kernels, layer(): pl.pallas_call(functools.partial(layer_kernel, levels, groups, patches),...  116 us
    pallas_call x1, Pallas kernels, attention_back(): pl.pallas_call(attention_kernel, grid=(WIDE,), out_shape=(jax.ShapeDtypeS...  7.77 us

profile of v3, /device:TPU:6, one launch (start us, length us, event | category | flops | bytes accessed | tf_op | source)
XLA Modules:
  0.0 124.6 jit_solution(13869695869328297418)
XLA Ops:
  0.6 116.2 %layer.1 = (f32[16,128,128]{2,1,0:T(8,128)}, bf16[16,128]{1,0:T(8,128)(2,1)}, bf16[128,2048]{1,0:T(8,128)(2,1)}, bf16[128,2048]{1,0:T(8,128)(2,1)}, bf16[128,204...) custom-call(bf16[32,4,2048]{2,1,0:T(4,128)(2,1)} %query_ref.1, bf16[32,4,2048]{2,1,0:T(4,128)(2,1)} %key_ref.1, ...), custom_call_target="tpu_custom_call" | custom-call | tf_op jit(solution)/shard_map/layer/pallas_call | solution.py:559
  116.8 7.8 %attention_back.1 = (bf16[32,4,2048]{2,1,0:T(4,128)(2,1)}, bf16[32,4,2048]{2,1,0:T(4,128)(2,1)}, bf16[32,4,2048]{2,1,0:T(4,128)(2,1)}) custom-call(bf16[128,2048]{1,0:T(8,128)(2,1)} %get-tuple-element.10.query_ref, bf16[128,2048]{1,0:T(8,128)(2,1)} %get-tuple-element.11.key_ref, bf16[128,2048]{1,0:T(8,128)(2,1)} %get-tuple-element.12.value_ref, ...), custom_call_target="tpu_custom_call" | custom-call | tf_op jit(solution)/shard_map/attention_back/pallas_call | solution.py:649

commit v4 on v3

--- a/solution.py
+++ b/solution.py
@@ -29,6 +29,7 @@
 PIECES = 2
 CHUNKS = 4
 WIDE = 4
+EARLY = 2
 
 
 def bits(n):
@@ -72,14 +73,15 @@
     probs_ref, onehot_ref, stream_ref, query_rows_ref, key_rows_ref, value_rows_ref, back_ref,
     query, key, value, mixed, cot_rows, probs_all, onehot_all, picked, returned, final_rows,
     gathered, w1, w2, own, x_send, x_recv, slopes, parts, cross, ring_in, ring_out,
-    last_in, gauge,
+    last_in, far_in, gauge,
     local_sem, load_sem, out_sem, own_sem, weight_send, weight_recv,
     ring_send, ring_recv, core_send, core_recv, x_send_sem, x_recv_sem,
-    slope_send, slope_recv, part_send, part_recv, back_send, back_recv, last_recv,
+    slope_send, slope_recv, part_send, part_recv, back_send, back_recv, last_recv, jump_recv,
     cot_send, cot_recv, pick_send, pick_recv, return_send, return_recv,
 ):
     steps = levels // 2
     last = steps - 1
+    near = steps * 5 // 8
     columns = 2 * levels
     frames, blocks, features = query_ref.shape
     local_rows = frames * blocks
@@ -140,7 +142,6 @@
     far = pl.ds(pl.multiple_of(block + core * share, share), share)
     other_far = pl.ds(pl.multiple_of(block + (1 - core) * share, share), share)
 
-    ring_in[last - 1] = jnp.zeros(ring_in.shape[1:], ring_in.dtype)
     pl.semaphore_wait(barrier, columns - 1 + 2 * (groups - 1))
 
     def cot_copy(other):
@@ -389,12 +390,80 @@
             part_last().start()
             part_own().start()
 
+    piece = block // CHUNKS
+
+    def chunk_of(q):
+        where = (1 - core) if q < CHUNKS // 2 else core
+        return where * share + (q % (CHUNKS // 2)) * piece
+
+    def back_copy(t, q):
+        chunk = pl.ds(pl.multiple_of(chunk_of(q), piece), piece)
+        return remote(
+            ring_out.at[t, chunk], ring_in.at[t - 1, chunk], back_send.at[0], back_recv.at[t, q], behind
+        )
+
+    def back_final(q):
+        chunk = pl.ds(pl.multiple_of(chunk_of(q), piece), piece)
+        n = q % (CHUNKS // 2)
+        owner = (1 - core) if q < CHUNKS // 2 else core
+        return remote(
+            ring_out.at[0, chunk], last_in.at[core, pl.ds(n * piece, piece)],
+            back_send.at[0], last_recv.at[core, n], (grp, behind[1] - core + owner),
+        )
+
+    def jump(q):
+        chunk = pl.ds(pl.multiple_of(chunk_of(q), piece), piece)
+        n = q % (CHUNKS // 2)
+        owner = (1 - core) if q < CHUNKS // 2 else core
+        home = lax.rem(level + levels - turn * (near + 1), levels)
+        return remote(
+            ring_out.at[near, chunk], far_in.at[core, pl.ds(n * piece, piece)],
+            back_send.at[0], jump_recv.at[core, n], (grp, 2 * home + owner),
+        )
+
+    def arrival(buffer, sem, way, n):
+        ref = buffer.at[way, pl.ds(n * piece, piece)]
+        return remote(ref, ref, back_send.at[0], sem.at[way, n], twin)
+
+    def scatter_first():
+        part_last().wait_recv()
+        for q in range(CHUNKS // 2, CHUNKS):
+            chunk = pl.ds(pl.multiple_of(chunk_of(q), piece), piece)
+            source = pl.ds(pl.multiple_of(block + chunk_of(q), piece), piece)
+            other = pl.ds((q - CHUNKS // 2) * piece, piece)
+            total = parts[last, source].astype(jnp.float32) + cross[last, other].astype(jnp.float32)
+            ring_out[last, chunk] = total.astype(jnp.bfloat16)
+            back_copy(last, q).start()
+
+    def scatter(t):
+        part_copy(t).wait_recv()
+        for q in range(CHUNKS):
+            chunk = pl.ds(pl.multiple_of(chunk_of(q), piece), piece)
+            source = pl.ds(pl.multiple_of(core * block + chunk_of(q), piece), piece)
+            total = parts[t, source].astype(jnp.float32) + cross[t, chunk].astype(jnp.float32)
+            begun = t == near - 1 or (t == last - 1 and q < CHUNKS // 2)
+            if not begun:
+                back_copy(t + 1, q).wait_recv()
+                total = total + ring_in[t, chunk].astype(jnp.float32)
+            ring_out[t, chunk] = total.astype(jnp.bfloat16)
+            if t == near:
+                jump(q).start()
+            elif t == 0:
+                back_final(q).start()
+            else:
+                back_copy(t, q).start()
+
     @pl.loop(0, steps + LAG_OUT)
     def _(i):
         for k in range(PIECES):
             advance(i, 1, k)
             advance(i + LEAD, 0, k)
 
+        if EARLY > 0 and near > 0:
+            @pl.when(i == steps + 1)
+            def _():
+                scatter(near - 1)
+
         @pl.when((i >= LAG_MID) & (i < steps + LAG_MID))
         def _():
             bend(i - LAG_MID)
@@ -402,6 +471,11 @@
         @pl.when(i >= LAG_OUT)
         def _():
             project(i - LAG_OUT)
+
+        if EARLY > 1 and near > 1:
+            @pl.when(i == steps + 2)
+            def _():
+                scatter(near - 2)
 
         @pl.when(i == 0)
         def _():
@@ -421,65 +495,15 @@
         def _():
             multiply(i)
 
-    piece = block // CHUNKS
-
-    def chunk_of(q):
-        where = (1 - core) if q < CHUNKS // 2 else core
-        return where * share + (q % (CHUNKS // 2)) * piece
-
-    def back_copy(t, q):
-        chunk = pl.ds(pl.multiple_of(chunk_of(q), piece), piece)
-        return remote(
-            ring_out.at[t, chunk], ring_in.at[lax.max(t - 1, 0), chunk], back_send.at[0], back_recv.at[t, q], behind
-        )
-
-    def back_final(q):
-        chunk = pl.ds(pl.multiple_of(chunk_of(q), piece), piece)
-        n = q % (CHUNKS // 2)
-        owner = (1 - core) if q < CHUNKS // 2 else core
-        return remote(
-            ring_out.at[0, chunk], last_in.at[core, pl.ds(n * piece, piece)],
-            back_send.at[0], last_recv.at[core, n], (grp, behind[1] - core + owner),
-        )
-
-    def back_arrival(way, n):
-        return remote(
-            ring_out.at[0, pl.ds(0, piece)], last_in.at[way, pl.ds(n * piece, piece)],
-            back_send.at[0], last_recv.at[way, n], ahead,
-        )
-
-    part_last().wait_recv()
-    for q in range(CHUNKS // 2, CHUNKS):
-        chunk = pl.ds(pl.multiple_of(chunk_of(q), piece), piece)
-        source = pl.ds(pl.multiple_of(block + chunk_of(q), piece), piece)
-        other = pl.ds((q - CHUNKS // 2) * piece, piece)
-        total = parts[last, source].astype(jnp.float32) + cross[last, other].astype(jnp.float32)
-        ring_out[last, chunk] = total.astype(jnp.bfloat16)
-        back_copy(last, q).start()
-
-    @pl.loop(0, last)
-    def _(i):
-        t = last - 1 - i
-        part_copy(t).wait_recv()
-        for q in range(CHUNKS):
-            chunk = pl.ds(pl.multiple_of(chunk_of(q), piece), piece)
-            source = pl.ds(pl.multiple_of(core * block + chunk_of(q), piece), piece)
-            total = parts[t, source].astype(jnp.float32) + cross[t, chunk].astype(jnp.float32)
-            if q < CHUNKS // 2:
-                @pl.when(i > 0)
-                def _():
-                    back_copy(t + 1, q).wait_recv()
-            else:
-                back_copy(t + 1, q).wait_recv()
-            ring_out[t, chunk] = (total + ring_in[t, chunk].astype(jnp.float32)).astype(jnp.bfloat16)
-
-            @pl.when(t > 0)
-            def _():
-                back_copy(t, q).start()
-
-            @pl.when(t == 0)
-            def _():
-                back_final(q).start()
+    early = min(EARLY, near)
+    scatter_first()
+    far_steps = list(range(last - 1, near - 1, -1))
+    near_steps = list(range(near - 1 - early, -1, -1))
+    while far_steps or near_steps:
+        if near_steps:
+            scatter(near_steps.pop(0))
+        if far_steps:
+            scatter(far_steps.pop(0))
 
     def return_copy(to):
         return remote(
@@ -500,9 +524,10 @@
         other = pl.ds(share + n * piece, piece)
         chunk = pl.ds(n * piece, piece)
         total = parts[last, rows].astype(jnp.float32) + cross[last, other].astype(jnp.float32)
-        for way in range(2):
-            back_arrival(way, n).wait_recv()
-        total = total + last_in[0, chunk].astype(jnp.float32) + last_in[1, chunk].astype(jnp.float32)
+        for buffer, sem in ((last_in, last_recv), (far_in, jump_recv)):
+            for way in range(2):
+                arrival(buffer, sem, way, n).wait_recv()
+                total = total + buffer[way, chunk].astype(jnp.float32)
         final_rows[chunk] = total.astype(jnp.bfloat16)
 
         @pl.loop(0, reach)
@@ -592,11 +617,12 @@
             pltpu.VMEM((steps, block, half), bf16),
             pltpu.VMEM((steps, block, half), bf16),
             pltpu.VMEM((2, share, half), bf16),
+            pltpu.VMEM((2, share, half), bf16),
             pltpu.VMEM((32, 128, 128), jnp.float32),
             dma((3,)), dma((3,)), dma((6,)), dma((3,)), dma((1,)), dma((1,)),
             dma((1,)), dma((steps, 2, PIECES)), dma((1,)), dma((steps,)),
             dma((1,)), dma((steps,)), dma((1,)), dma((steps,)),
-            dma((1,)), dma((steps + 1,)), dma((1,)), dma((steps, CHUNKS)), dma((2, CHUNKS // 2)),
+            dma((1,)), dma((steps + 1,)), dma((1,)), dma((steps, CHUNKS)), dma((2, CHUNKS // 2)), dma((2, CHUNKS // 2)),
             dma((1,)), dma((1,)), dma((2,)), dma((2,)), dma((1,)), dma((1,)),
         ],
         compiler_params=pltpu.CompilerParams(
@@ -619,24 +645,37 @@
         onehot_ref[...], back_ref[...], TN_DIMS, preferred_element_type=jnp.float32
     )
     stream = (stream_ref[...].astype(jnp.float32) + added).astype(jnp.bfloat16)
+    cols = [slice(n * head_dim, (n + 1) * head_dim) for n in range(heads)]
+
+    def store(ref, n, values):
+        ref[:, :, cols[n]] = values.astype(jnp.bfloat16).reshape(frames, blocks, head_dim)
+
+    grad_probs = [
+        lax.dot_general(stream[:, c], value_ref[:, c], NT_DIMS, preferred_element_type=jnp.float32) for c in cols
+    ]
+    grad_values = [
+        lax.dot_general(
+            probs_ref[n].astype(jnp.bfloat16), stream[:, c], TN_DIMS, preferred_element_type=jnp.float32
+        ) for n, c in enumerate(cols)
+    ]
+    grad_scores = []
     for n in range(heads):
-        cols = slice(n * head_dim, (n + 1) * head_dim)
-        grad = stream[:, cols]
-        query = query_ref[:, cols]
-        key = key_ref[:, cols]
-        value = value_ref[:, cols]
-        probs = probs_ref[n]
-        grad_value = lax.dot_general(
-            probs.astype(jnp.bfloat16), grad, TN_DIMS, preferred_element_type=jnp.float32
-        )
-        grad_value_ref[:, :, cols] = grad_value.astype(jnp.bfloat16).reshape(frames, blocks, head_dim)
-        grad_prob = lax.dot_general(grad, value, NT_DIMS, preferred_element_type=jnp.float32)
-        centre = jnp.sum(probs * grad_prob, axis=1, keepdims=True)
-        grad_score = (probs * (grad_prob - centre)).astype(jnp.bfloat16)
-        grad_query = jnp.dot(grad_score, key, preferred_element_type=jnp.float32) * scaling
-        grad_query_ref[:, :, cols] = grad_query.astype(jnp.bfloat16).reshape(frames, blocks, head_dim)
-        grad_key = lax.dot_general(grad_score, query, TN_DIMS, preferred_element_type=jnp.float32) * scaling
-        grad_key_ref[:, :, cols] = grad_key.astype(jnp.bfloat16).reshape(frames, blocks, head_dim)
+        weighted = probs_ref[n] * grad_probs[n]
+        centre = jnp.sum(weighted, axis=1, keepdims=True)
+        grad_scores.append((probs_ref[n] * (grad_probs[n] - centre)).astype(jnp.bfloat16))
+    for n in range(heads):
+        store(grad_value_ref, n, grad_values[n])
+    grad_queries = [
+        jnp.dot(grad_scores[n], key_ref[:, c], preferred_element_type=jnp.float32) * scaling
+        for n, c in enumerate(cols)
+    ]
+    grad_keys = [
+        lax.dot_general(grad_scores[n], query_ref[:, c], TN_DIMS, preferred_element_type=jnp.float32) * scaling
+        for n, c in enumerate(cols)
+    ]
+    for n in range(heads):
+        store(grad_query_ref, n, grad_queries[n])
+        store(grad_key_ref, n, grad_keys[n])
 
 
 def attention_back(frames, query, key, value, probs, onehot, stream, back):

time: 125 us -> 116 us (0.928)
  Pallas kernels: 124 us -> 115 us
    pallas_call x1, Pallas kernels: 116 us -> 110 us  [layer(): pl.pallas_call(functools.partial(layer_kernel, levels, groups, patches),...]
    pallas_call x1, Pallas kernels: 7.77 us -> 5.15 us  [attention_back(): pl.pallas_call(attention_kernel, grid=(WIDE,), out_shape=(jax.ShapeDtypeS...]
where the time goes in v4:
time: 116 us
  Pallas kernels  115 us (99%)
    pallas_call x1, Pallas kernels, layer(): pl.pallas_call(functools.partial(layer_kernel, levels, groups, patches),...  110 us
    pallas_call x1, Pallas kernels, attention_back(): pl.pallas_call(attention_kernel, grid=(WIDE,), out_shape=(jax.ShapeDtypeS...  5.15 us

profile of v4, /device:TPU:6, one launch (start us, length us, event | category | flops | bytes accessed | tf_op | source)
XLA Modules:
  0.0 115.8 jit_solution(5447588713382953946)
XLA Ops:
  0.6 110.0 %layer.1 = (f32[16,128,128]{2,1,0:T(8,128)}, bf16[16,128]{1,0:T(8,128)(2,1)}, bf16[128,2048]{1,0:T(8,128)(2,1)}, bf16[128,2048]{1,0:T(8,128)(2,1)}, bf16[128,204...) custom-call(bf16[32,4,2048]{2,1,0:T(4,128)(2,1)} %query_ref.1, bf16[32,4,2048]{2,1,0:T(4,128)(2,1)} %key_ref.1, ...), custom_call_target="tpu_custom_call" | custom-call | tf_op jit(solution)/shard_map/layer/pallas_call | solution.py:584
  110.6 5.2 %attention_back.1 = (bf16[32,4,2048]{2,1,0:T(4,128)(2,1)}, bf16[32,4,2048]{2,1,0:T(4,128)(2,1)}, bf16[32,4,2048]{2,1,0:T(4,128)(2,1)}) custom-call(bf16[128,2048]{1,0:T(8,128)(2,1)} %get-tuple-element.10.query_ref, bf16[128,2048]{1,0:T(8,128)(2,1)} %get-tuple-element.11.key_ref, bf16[128,2048]{1,0:T(8,128)(2,1)} %get-tuple-element.12.value_ref, ...), custom_call_target="tpu_custom_call" | custom-call | tf_op jit(solution)/shard_map/attention_back/pallas_call | solution.py:688

commit v5 on v4

--- a/solution.py
+++ b/solution.py
@@ -26,9 +26,9 @@
 LAG_MID = 2
 LAG_OUT = 4
 LEAD = 1
-PIECES = 2
+PIECES = 4
 CHUNKS = 4
-WIDE = 4
+WIDE = 2
 EARLY = 2
 
 

time: 116 us -> 113 us (0.974)
  Pallas kernels: 115 us -> 113 us
    pallas_call x1, Pallas kernels: 110 us -> 109 us  [layer(): pl.pallas_call(functools.partial(layer_kernel, levels, groups, patches),...]
    pallas_call x1, Pallas kernels: 5.15 us -> 3.91 us  [attention_back(): pl.pallas_call(attention_kernel, grid=(WIDE,), out_shape=(jax.ShapeDtypeS...]
where the time goes in v5:
time: 113 us
  Pallas kernels  113 us (100%)
    pallas_call x1, Pallas kernels, layer(): pl.pallas_call(functools.partial(layer_kernel, levels, groups, patches),...  109 us
    pallas_call x1, Pallas kernels, attention_back(): pl.pallas_call(attention_kernel, grid=(WIDE,), out_shape=(jax.ShapeDtypeS...  3.91 us

profile of v5, /device:TPU:6, one launch (start us, length us, event | category | flops | bytes accessed | tf_op | source)
XLA Modules:
  0.0 113.2 jit_solution(13507882581156406419)
XLA Ops:
  0.6 108.7 %layer.1 = (f32[16,128,128]{2,1,0:T(8,128)}, bf16[16,128]{1,0:T(8,128)(2,1)}, bf16[128,2048]{1,0:T(8,128)(2,1)}, bf16[128,2048]{1,0:T(8,128)(2,1)}, bf16[128,204...) custom-call(bf16[32,4,2048]{2,1,0:T(4,128)(2,1)} %query_ref.1, bf16[32,4,2048]{2,1,0:T(4,128)(2,1)} %key_ref.1, ...), custom_call_target="tpu_custom_call" | custom-call | tf_op jit(solution)/shard_map/layer/pallas_call | solution.py:584
  109.3 3.9 %attention_back.1 = (bf16[32,4,2048]{2,1,0:T(4,128)(2,1)}, bf16[32,4,2048]{2,1,0:T(4,128)(2,1)}, bf16[32,4,2048]{2,1,0:T(4,128)(2,1)}) custom-call(bf16[128,2048]{1,0:T(8,128)(2,1)} %get-tuple-element.10.query_ref, bf16[128,2048]{1,0:T(8,128)(2,1)} %get-tuple-element.11.key_ref, bf16[128,2048]{1,0:T(8,128)(2,1)} %get-tuple-element.12.value_ref, ...), custom_call_target="tpu_custom_call" | custom-call | tf_op jit(solution)/shard_map/attention_back/pallas_call | solution.py:688
